TPU v7x, 128 devices: a whole 4x4x4 slice. The times are simulated.
128 devices in a mesh: ctx: 32 (over x, z, core), grp: 4 (over y).
Axes of the slice: x: 4, y: 4, z: 4, core: 2. Of those that a mesh axis runs over, the one named last changes fastest.
Arguments:
- query_heads: bfloat16 [16384, 2048], P('ctx', 'grp'), may hold values from -6 to 6
- key_heads: bfloat16 [16384, 2048], P('ctx', 'grp'), may hold values from -6 to 6
- value_heads: bfloat16 [16384, 2048], P('ctx', 'grp'), may hold values from -6 to 6
- log_decay: float32 [16, 16384], P('grp', 'ctx'), may hold values from -1 to 0
- residual: bfloat16 [16384, 2048], P(('ctx', 'grp')), may hold values from -4 to 4
- out_weight: bfloat16 [2048, 2048], replicated, may hold values from -0.5 to 0.5
- norm_gain: float32 [2048], replicated, may hold values from 0.25 to 1.75
- expert_ids: int32 [16384, 6], P(('ctx', 'grp')), may hold values from 0 to 63, all different within a row; in each aligned block of 128 rows (0 to 127, 128 to 255, ...) at most 15 rows name the same one
- gate_weights: float32 [16384, 6], P(('ctx', 'grp')), may hold values from 0.1 to 1
- gate_proj: bfloat16 [64, 2048, 1408], P('ctx', None, 'grp'), may hold values from -0.125 to 0.125
- up_proj: bfloat16 [64, 2048, 1408], P('ctx', None, 'grp'), may hold values from -0.125 to 0.125
- down_proj: bfloat16 [64, 1408, 2048], P('ctx', 'grp'), may hold values from -0.15625 to 0.15625
Outputs:
- attended: bfloat16 [16384, 2048], P(('ctx', 'grp'))
- layer_out: bfloat16 [16384, 2048], P(('ctx', 'grp'))
Inputs may be any that keep to these rules, and one draw needn't show every extreme that they name: `expert_ids`: each token names 6 different experts. In each aligned block of 128 tokens no expert is named by more than 15 tokens, and that bound is reached.
All inputs are finite; a program needn't handle non-finite values.
Results may differ from a plain program's by a relative error of at most 0.02.
Values may be sent and summed in bfloat16 or wider, within the bound.
No kernel may reach another device: no remote copies, remote signals or barrier semaphores. Data moves between devices by JAX's collectives and lax.ppermute only.
A program may use at most 128 MiB of HBM per device.

v0:
```python
import functools

import jax
import jax.numpy as jnp
from jax import lax
from jax.experimental import pallas as pl
from jax.experimental.pallas import tpu as pltpu
from jax.sharding import PartitionSpec as P


D = 2048
HD = 128
E = 64
TOPK = 6
SLOTS = 16
CHUNKS = 2
EXTRA = 8
GRANT = 58 << 20
FAR = [(0, 3), (3, 0), (1, 2), (2, 1)]
NEAR = [(0, 1), (1, 0), (2, 3), (3, 2)]
F32 = jnp.float32
BF16 = jnp.bfloat16


def feature(values):
    wide = values.astype(F32)
    return jnp.where(wide > 0, wide + 1.0, jnp.exp(jnp.minimum(wide, 0.0))).astype(BF16)


def running_sum(rows):
    lanes = lax.broadcasted_iota(jnp.int32, rows.shape, 1)
    step = 1
    while step < rows.shape[1]:
        rows = rows + jnp.where(lanes >= step, pltpu.roll(rows, step, 1), 0.0)
        step *= 2
    return rows


def padded_decay(decay_ref):
    decay = decay_ref[...]
    return jnp.concatenate([decay, jnp.zeros((8 - decay.shape[0], decay.shape[1]), F32)], axis=0)


def state_body(k_ref, v_ref, decay_ref, out_ref):
    heads, length = decay_ref.shape
    cum = running_sum(padded_decay(decay_ref))
    total = cum[:, length - 1 :]
    fade = jnp.exp(total - cum).T
    parts = out_ref.shape[0] // heads
    row = lax.broadcasted_iota(jnp.int32, (EXTRA, HD), 0)
    for h in range(heads):
        cols = slice(h * HD, (h + 1) * HD)
        tail = feature(k_ref[:, cols]).astype(F32) * fade[:, h : h + 1]
        norm = jnp.sum(tail, axis=0, keepdims=True)
        state = lax.dot_general(
            tail.astype(BF16), v_ref[:, cols], (((0,), (0,)), ((), ())), preferred_element_type=F32
        )
        out_ref[h * parts : (h + 1) * parts, 0:SLOTS, :] = state.astype(BF16).reshape(
            parts, SLOTS, HD
        )
        norm_hi = norm.astype(BF16).astype(F32)
        tot = jnp.broadcast_to(total[h : h + 1, :], (1, HD))
        tot_hi = tot.astype(BF16).astype(F32)
        tot_lo = (tot - tot_hi).astype(BF16).astype(F32)
        extra = jnp.zeros((EXTRA, HD), F32)
        for i, line in enumerate((norm_hi, norm - norm_hi, tot_hi, tot_lo, tot - tot_hi - tot_lo)):
            extra = jnp.where(row == i, line, extra)
        out_ref[h * parts : (h + 1) * parts, SLOTS:, :] = jnp.broadcast_to(
            extra.astype(BF16)[None], (parts, EXTRA, HD)
        )


def local_states(keys, values, decay, blocks):
    return pl.pallas_call(
        state_body,
        out_shape=jax.ShapeDtypeStruct((blocks, SLOTS + EXTRA, HD), BF16),
        compiler_params=pltpu.CompilerParams(vmem_limit_bytes=GRANT),
        name="local_states",
    )(keys, values, decay)


def prior_body(got_ref, out_ref):
    blocks = got_ref.shape[0]
    row = lax.broadcasted_iota(jnp.int32, (EXTRA, HD), 0)

    def step(b, carry):
        state, norm = carry
        extra = got_ref[b, SLOTS:, :].astype(F32)

        def line(i):
            return jnp.sum(jnp.where(row == i, extra, 0.0), axis=0, keepdims=True)

        norm_hi = norm.astype(BF16).astype(F32)
        out_ref[b, 0:SLOTS, :] = state.astype(BF16)
        out_ref[b, SLOTS:, :] = jnp.where(
            row == 0, norm_hi, jnp.where(row == 1, norm - norm_hi, 0.0)
        ).astype(BF16)
        fade = jnp.exp(line(2) + line(3) + line(4))
        state = fade * state + got_ref[b, 0:SLOTS, :].astype(F32)
        norm = fade * norm + line(0) + line(1)
        return state, norm

    lax.fori_loop(
        0, blocks, step, (jnp.zeros((SLOTS, HD), F32), jnp.zeros((1, HD), F32)), unroll=4
    )


def prior_states(got):
    return pl.pallas_call(
        prior_body, out_shape=jax.ShapeDtypeStruct(got.shape, BF16), compiler_params=pltpu.CompilerParams(vmem_limit_bytes=4 << 20),
        name="prior_states"
    )(got)


def inner_body(q_ref, k_ref, v_ref, decay_ref, num_ref, den_ref):
    heads, length = decay_ref.shape
    cum = running_sum(padded_decay(decay_ref))
    cum_col = cum.T
    tile = 128
    lane = lax.broadcasted_iota(jnp.int32, (tile, HD), 1)
    for t in range(length // tile):
        rows = slice(t * tile, (t + 1) * tile)
        seen = (t + 1) * tile
        col = lax.broadcasted_iota(jnp.int32, (tile, seen), 1)
        at = lax.broadcasted_iota(jnp.int32, (tile, seen), 0) + t * tile
        causal = col <= at
        dens = jnp.zeros((tile, HD), F32)
        for h in range(heads):
            cols = slice(h * HD, (h + 1) * HD)
            scores = lax.dot_general(
                feature(q_ref[rows, cols]),
                feature(k_ref[0:seen, cols]),
                (((1,), (1,)), ((), ())),
                preferred_element_type=F32,
            )
            spread = cum_col[rows, h : h + 1] - cum[h : h + 1, 0:seen]
            weights = jnp.where(causal, scores * jnp.exp(jnp.where(causal, spread, 0.0)), 0.0)
            dens = jnp.where(lane == h, jnp.sum(weights, axis=1, keepdims=True), dens)
            num_ref[rows, cols] = jnp.dot(
                weights.astype(BF16), v_ref[0:seen, cols], preferred_element_type=F32
            )
        den_ref[rows, :] = dens


def inner_attention(queries, keys, values, decay):
    length, width = queries.shape
    return pl.pallas_call(
        inner_body,
        out_shape=[
            jax.ShapeDtypeStruct((length, width), F32),
            jax.ShapeDtypeStruct((length, HD), F32),
        ],
        cost_estimate=pl.CostEstimate(
            flops=4 * length * length * width,
            bytes_accessed=8 * length * width,
            transcendentals=4 * length * length,
        ),
        compiler_params=pltpu.CompilerParams(vmem_limit_bytes=GRANT),
        name="inner_attention",
    )(queries, keys, values, decay)


def outer_body(q_ref, decay_ref, prior_ref, num_ref, den_ref, out_ref):
    heads, length = decay_ref.shape
    groups = out_ref.shape[0]
    parts = prior_ref.shape[0] // heads
    damp = jnp.exp(running_sum(padded_decay(decay_ref))).T
    row = lax.broadcasted_iota(jnp.int32, (EXTRA, HD), 0)
    for h in range(heads):
        cols = slice(h * HD, (h + 1) * HD)
        feat = feature(q_ref[:, cols])
        state = prior_ref[h * parts : (h + 1) * parts, 0:SLOTS, :].reshape(HD, HD)
        extra = prior_ref[h * parts, SLOTS:, :].astype(F32)
        norm = jnp.sum(jnp.where(row < 2, extra, 0.0), axis=0, keepdims=True)
        scale = damp[:, h : h + 1]
        num = num_ref[:, cols] + scale * jnp.dot(feat, state, preferred_element_type=F32)
        den = den_ref[:, h : h + 1] + scale * jnp.sum(
            feat.astype(F32) * norm, axis=1, keepdims=True
        )
        out_ref[:, :, cols] = (num / den).astype(BF16).reshape(groups, length // groups, HD)


def outer_attention(queries, decay, prior, num, den, groups):
    length, width = queries.shape
    return pl.pallas_call(
        outer_body,
        out_shape=jax.ShapeDtypeStruct((groups, length // groups, width), BF16),
        compiler_params=pltpu.CompilerParams(vmem_limit_bytes=GRANT),
        name="outer_attention",
    )(queries, decay, prior, num, den)


def route_body(ids_ref, gates_ref, dispatch_ref, combine_ref, even_ref, odd_ref):
    rows = ids_ref.shape[1]
    expert = lax.broadcasted_iota(jnp.int32, (E, rows), 0)
    hits = jnp.zeros((E, rows), F32)
    gates = jnp.zeros((E, rows), F32)
    for k in range(TOPK):
        match = expert == ids_ref[k : k + 1, :]
        hits = jnp.where(match, 1.0, hits)
        gates = jnp.where(match, gates_ref[k : k + 1, :], gates)
    before = (
        lax.broadcasted_iota(jnp.int32, (rows, rows), 0)
        < lax.broadcasted_iota(jnp.int32, (rows, rows), 1)
    ).astype(BF16)
    slot = jnp.dot(hits.astype(BF16), before, preferred_element_type=F32)
    slot = jnp.where(hits > 0.0, slot, -1.0)
    gates = gates.astype(BF16).astype(F32)
    half = SLOTS // CHUNKS
    for chunk in range(CHUNKS):
        place = lax.broadcasted_iota(jnp.int32, (E, half, rows), 1) + chunk * half
        here = jnp.broadcast_to(slot[:, None, :], (E, half, rows)) == place.astype(F32)
        dispatch_ref[chunk] = jnp.where(here, 1.0, 0.0).reshape(E * half, rows).astype(BF16)
        mix = jnp.where(here, jnp.broadcast_to(gates[:, None, :], (E, half, rows)), 0.0)
        combine_ref[chunk] = mix.reshape(E * half, rows).astype(BF16)
        if chunk == 0:
            by_parity = mix.reshape(E // 2, 2, half, rows)
            for parity, ref in ((0, even_ref), (1, odd_ref)):
                ref[...] = by_parity[:, parity].reshape(E // 2 * half, rows).astype(BF16)


def route(ids, gates):
    rows = ids.shape[1]
    shape = jax.ShapeDtypeStruct((CHUNKS, E * SLOTS // CHUNKS, rows), BF16)
    part = jax.ShapeDtypeStruct((E // 2 * SLOTS // CHUNKS, rows), BF16)
    return pl.pallas_call(
        route_body,
        out_shape=[shape, shape, part, part], compiler_params=pltpu.CompilerParams(vmem_limit_bytes=4 << 20),
        name="route",
    )(ids, gates)


def contract_last(x, y):
    return lax.dot_general(x, y, (((1,), (1,)), ((), ())), preferred_element_type=F32)


def apply_half(x, weights, store, waits):
    waits(0)
    gate = contract_last(x, weights[0])
    waits(1)
    up = contract_last(x, weights[1])
    hidden = (jax.nn.silu(gate) * up).astype(BF16)
    waits(2)
    width = D // 4

    def down(i, carry):
        at = pl.multiple_of(i * width, width)
        store(at, width, jnp.dot(hidden, weights[2, :, pl.ds(at, width)], preferred_element_type=F32))
        return carry

    lax.fori_loop(0, 4, down, 0)


def single_body(which, x_ref, g_ref, u_ref, d_ref, gf, uf, df, out_ref, xs, ws, sems):
    quarter = gf.shape[0]
    copies = []
    for i, (own, far) in enumerate(((g_ref, gf), (u_ref, uf), (d_ref, df))):
        copies.append(
            (
                pltpu.make_async_copy(own.at[which], ws.at[i, 0:quarter], sems.at[2 * i]),
                pltpu.make_async_copy(far, ws.at[i, quarter : 2 * quarter], sems.at[2 * i + 1]),
            )
        )
    x_copy = pltpu.make_async_copy(x_ref, xs, sems.at[6])
    x_copy.start()
    for pair in copies:
        for copy in pair:
            copy.start()
    x_copy.wait()

    def waits(i):
        for copy in copies[i]:
            copy.wait()

    def store(at, width, value):
        out_ref[:, pl.ds(at, width)] = value.astype(BF16)

    apply_half(xs[...].reshape(-1, D), ws, store, waits)


def single_ffn(x, own, far, which):
    quarter = far[0].shape[0]
    blocks, rows, _ = x.shape
    total = blocks * rows
    anywhere = pl.BlockSpec(memory_space=pl.ANY)
    held = pl.BlockSpec(memory_space=pltpu.HBM)
    return pl.pallas_call(
        functools.partial(single_body, which),
        out_shape=jax.ShapeDtypeStruct((total, D), BF16),
        in_specs=[anywhere] + [held] * 6,
        out_specs=pl.BlockSpec(memory_space=pltpu.VMEM),
        scratch_shapes=[
            pltpu.VMEM((blocks, rows, D), BF16),
            pltpu.VMEM((3, 2 * quarter, D), BF16),
            pltpu.SemaphoreType.DMA((7,)),
        ],
        compiler_params=pltpu.CompilerParams(vmem_limit_bytes=GRANT),
        cost_estimate=pl.CostEstimate(
            flops=12 * total * quarter * D,
            bytes_accessed=12 * quarter * D + 4 * total * D,
            transcendentals=2 * total * quarter,
        ),
        name="single_ffn",
    )(x, *own, *far)


def pair_body(starts, xa, xb, g_ref, u_ref, d_ref, ga, ua, da, gb, ub, db, out_ref, xs, ws, sems):
    quarter = ga.shape[0]
    blocks, rows, _ = out_ref.shape
    rows = rows // 2
    for e, (x_ref, fars) in enumerate(((xa, (ga, ua, da)), (xb, (gb, ub, db)))):
        pltpu.make_async_copy(
            x_ref.at[:, starts[e] : starts[e] + rows, :], xs.at[e], sems.at[7 * e + 6]
        ).start()
        for i, (own, far) in enumerate(zip((g_ref, u_ref, d_ref), fars)):
            pair = (
                pltpu.make_async_copy(own.at[e], ws.at[e, i, 0:quarter], sems.at[7 * e + 2 * i]),
                pltpu.make_async_copy(
                    far, ws.at[e, i, quarter : 2 * quarter], sems.at[7 * e + 2 * i + 1]
                ),
            )
            for copy in pair:
                copy.start()

    def expert(e, carry):
        def wait_for(ref, dst, sem):
            pltpu.make_async_copy(ref, dst, sems.at[7 * e + sem]).wait()

        wait_for(xa.at[:, 0:rows, :], xs.at[e], 6)

        def waits(i):
            wait_for(ga, ws.at[e, i, 0:quarter], 2 * i)
            wait_for(ga, ws.at[e, i, quarter : 2 * quarter], 2 * i + 1)

        def store(at, width, value):
            where = pl.ds(pl.multiple_of(e * rows, rows), rows)
            out_ref[:, where, pl.ds(at, width)] = value.astype(BF16).reshape(blocks, rows, width)

        apply_half(xs[e].reshape(-1, D), ws.at[e], store, waits)
        return carry

    lax.fori_loop(0, 2, expert, 0)


def pair_ffn(xa, xb, starts, own, fars):
    quarter = fars[0][0].shape[0]
    blocks = xa.shape[0]
    rows = SLOTS // CHUNKS
    total = 2 * blocks * rows
    anywhere = pl.BlockSpec(memory_space=pl.ANY)
    held = pl.BlockSpec(memory_space=pltpu.HBM)
    return pl.pallas_call(
        functools.partial(pair_body, starts),
        out_shape=jax.ShapeDtypeStruct((blocks, 2 * rows, D), BF16),
        in_specs=[anywhere] * 2 + [held] * 9,
        out_specs=pl.BlockSpec(memory_space=pltpu.VMEM),
        scratch_shapes=[
            pltpu.VMEM((2, blocks, rows, D), BF16),
            pltpu.VMEM((2, 3, 2 * quarter, D), BF16),
            pltpu.SemaphoreType.DMA((14,)),
        ],
        compiler_params=pltpu.CompilerParams(vmem_limit_bytes=GRANT),
        cost_estimate=pl.CostEstimate(
            flops=12 * total * quarter * D,
            bytes_accessed=24 * quarter * D + 4 * total * D,
            transcendentals=2 * total * quarter,
        ),
        name="pair_ffn",
    )(xa, xb, *own, *fars[0], *fars[1])


def merge_body(own, came_a, came_b, out):
    blocks, rows, _ = out.shape
    rows = rows // 2
    for at, came in ((0, came_a), (rows, came_b)):
        back = came[...].astype(F32).reshape(blocks, rows, D)
        out[:, at : at + rows, :] = (own[:, at : at + rows, :].astype(F32) + back).astype(BF16)


def merge(own, came_a, came_b):
    blocks, rows, _ = own.shape
    steps = 4
    wide = pl.BlockSpec((blocks // steps, rows, D), lambda i: (i, 0, 0))
    flat = pl.BlockSpec((came_a.shape[0] // steps, D), lambda i: (i, 0))
    return pl.pallas_call(
        merge_body,
        grid=(steps,),
        out_shape=jax.ShapeDtypeStruct(own.shape, BF16),
        in_specs=[wide, flat, flat],
        out_specs=wide,
        compiler_params=pltpu.CompilerParams(vmem_limit_bytes=16 << 20),
        cost_estimate=pl.CostEstimate(
            flops=blocks * rows * D, bytes_accessed=6 * blocks * rows * D, transcendentals=0
        ),
        name="merge",
    )(own, came_a, came_b)


def partner_body(back, mix_a, mix_b, far_ref, near_ref):
    blocks, rows, width = back.shape
    rows = rows // 2
    for at, mix, out in ((0, mix_a, far_ref), (rows, mix_b, near_ref)):
        part = back[:, at : at + rows, :].reshape(blocks * rows, width)
        out[...] = lax.dot_general(
            mix[...], part, (((0,), (0,)), ((), ())), preferred_element_type=F32
        ).astype(BF16)


def partner_mix(back, mix_a, mix_b):
    blocks, rows, _ = back.shape
    tokens = mix_a.shape[1]
    steps = 4
    out = jax.ShapeDtypeStruct((tokens, D), BF16)
    whole = pl.BlockSpec(mix_a.shape, lambda i: (0, 0))
    strip = pl.BlockSpec((tokens, D // steps), lambda i: (0, i))
    return pl.pallas_call(
        partner_body,
        grid=(steps,),
        out_shape=[out, out],
        in_specs=[
            pl.BlockSpec((blocks, rows, D // steps), lambda i: (0, 0, i)),
            whole,
            whole,
        ],
        out_specs=[strip, strip],
        compiler_params=pltpu.CompilerParams(vmem_limit_bytes=16 << 20),
        cost_estimate=pl.CostEstimate(
            flops=2 * blocks * rows * tokens * D,
            bytes_accessed=2 * blocks * rows * D,
            transcendentals=0,
        ),
        name="partner_mix",
    )(back, mix_a, mix_b)


def on_device(
    query_heads,
    key_heads,
    value_heads,
    log_decay,
    residual,
    out_weight,
    norm_gain,
    expert_ids,
    gate_weights,
    gate_proj,
    up_proj,
    down_proj,
):
    n_ctx = lax.axis_size("ctx")
    gate_t = jnp.swapaxes(gate_proj, 1, 2)
    up_t = jnp.swapaxes(up_proj, 1, 2)
    pairs = ((NEAR, FAR), (FAR, NEAR))
    own_w = (gate_t, up_t, down_proj)
    far_w = [[], []]
    for w in (gate_t, up_t, down_proj):
        for which in range(2):
            far_w[which].append(lax.ppermute(w[which], "grp", pairs[which][0]))

    n_grp = lax.axis_size("grp")
    payload = local_states(key_heads, value_heads, log_decay, n_ctx)
    got = lax.all_to_all(payload, "ctx", 0, 0, tiled=True)
    dispatch, combine, even, odd = route(jnp.swapaxes(expert_ids, 0, 1), jnp.swapaxes(gate_weights, 0, 1))
    far_even = lax.ppermute(even, "grp", FAR)
    near_odd = lax.ppermute(odd, "grp", NEAR)
    back = prior_states(got)
    prior = lax.all_to_all(back, "ctx", 0, 0, tiled=True)
    num, den = inner_attention(query_heads, key_heads, value_heads, log_decay)
    mixed = outer_attention(query_heads, log_decay, prior, num, den, n_grp)
    heads_in = lax.all_to_all(mixed, "grp", 0, 0, tiled=True)
    projected = jnp.einsum(
        "gtc,gcd->td", heads_in, out_weight.reshape(n_grp, -1, D), preferred_element_type=F32
    )
    attended = (residual.astype(F32) + projected).astype(BF16)
    widened = attended.astype(F32)
    normed = (
        widened * lax.rsqrt(jnp.mean(widened * widened, axis=1, keepdims=True) + 1e-06) * norm_gain
    ).astype(BF16)

    half = SLOTS // CHUNKS
    sent = []
    for chunk in range(CHUNKS):
        buffer = jnp.dot(dispatch[chunk], normed, preferred_element_type=F32).astype(BF16)
        sent.append(
            lax.all_to_all(buffer.reshape(n_ctx, 2 * half, D), "ctx", 0, 0, tiled=True)
        )
    others = []
    for chunk in range(CHUNKS):
        for which in range(2):
            own = sent[chunk][:, which * half : (which + 1) * half]
            others.append(lax.ppermute(own, "grp", pairs[which][1]))

    def home(rows):
        return lax.all_to_all(rows, "ctx", 0, 0, tiled=True)

    def mix(chunk, back):
        return lax.dot_general(
            combine[chunk],
            back.reshape(-1, D),
            (((0,), (0,)), ((), ())),
            preferred_element_type=F32,
        )

    own0 = pair_ffn(sent[0], sent[0], (0, half), own_w, far_w)
    back_own0 = home(own0)
    other0 = pair_ffn(others[0], others[1], (0, 0), own_w, far_w)
    back_other0 = home(other0)
    for_far, for_near = partner_mix(back_other0, far_even, near_odd)
    from_far = lax.ppermute(for_far, "grp", FAR)
    from_near = lax.ppermute(for_near, "grp", NEAR)

    own1 = pair_ffn(sent[1], sent[1], (0, half), own_w, far_w)
    came = []
    for which in range(2):
        other = single_ffn(others[2 + which], own_w, far_w[which], which)
        came.append(lax.ppermute(other, "grp", pairs[which][1]))
    back1 = home(merge(own1, *came))
    total = widened + mix(0, back_own0) + from_far.astype(F32) + from_near.astype(F32)
    total = total + mix(1, back1)
    return (attended, total.astype(BF16))


def solution(mesh):
    placed = (
        P("ctx", "grp"),
        P("ctx", "grp"),
        P("ctx", "grp"),
        P("grp", "ctx"),
        P(("ctx", "grp"), None),
        P(),
        P(),
        P(("ctx", "grp"), None),
        P(("ctx", "grp"), None),
        P("ctx", None, "grp"),
        P("ctx", None, "grp"),
        P("ctx", "grp", None),
    )

    return jax.shard_map(
        on_device,
        mesh=mesh,
        in_specs=placed,
        out_specs=(P(("ctx", "grp"), None), P(("ctx", "grp"), None)),
        check_vma=False,
    )
```

profile of v0, /device:TPU:1, one launch (start us, length us, event | category | flops | bytes accessed | tf_op | source)
XLA Modules:
  0.0 360.5 jit_solution(13329963593670980189)
XLA Ops:
  0.6 3.3 local_states.1
  3.9 17.7 %all_to_all.40.got_ref = bf16[32,24,128]{2,1,0:T(8,128)(2,1)S(1)} all-to-all(bf16[32,24,128]{2,1,0:T(8,128)(2,1)} %local_states.1), channel_id=1, replica_groups=mesh['ctx'=32,'grp'=4] {'ctx'}, dimensions={0} | all-to-all | bytes 393216 | tf_op jit(solution)/shard_map/all_to_all | solution.py:462
  22.6 3.8 %all-to-all-start.1 = ((bf16[32,24,128]{2,1,0:T(8,128)(2,1)}), bf16[32,24,128]{2,1,0:T(8,128)(2,1)S(1)}, u32[]{:S(2)}, u32[]{:S(2)}) async-start(bf16[32,24,128]{2,1,0:T(8,128)(2,1)} %prior_states.1), calls=%async_computation.1 | async-start | bytes 393216 | tf_op jit(solution)/shard_map/all_to_all | solution.py:467
  26.4 5.6 %inner_attention.1 = (f32[512,512]{1,0:T(8,128)}, f32[512,128]{1,0:T(8,128)}) custom-call(bf16[512,512]{1,0:T(8,128)(2,1)} %q_ref.3, bf16[512,512]{1,0:T(8,128)(2,1)} %k_ref.3, bf16[512,512]{1,0:T(8,128)(2,1)} %v_ref.3, f32[4,512]{1,0:T(4,128)} %decay_ref.5), custom_call_target="tpu_custom_call" | custom-call | flops 536870912 | bytes 2097152 | tf_op jit(solution)/shard_map/inner_attention/pallas_call | solution.py:147
  32.0 2.8 all-to-all-done.1.prior_ref
  35.5 3.9 %outer_attention.1 = bf16[4,128,512]{2,1,0:T(8,128)(2,1)} custom-call(bf16[512,512]{1,0:T(8,128)(2,1)} %q_ref.3, f32[4,512]{1,0:T(4,128)} %decay_ref.5, bf16[32,24,128]{2,1,0:T(8,128)(2,1)} %copy-done.13, f32[512,512]{1,0:T(8,128)} %get-tuple-element.10.num_ref, f32[512,128]{1,0:T(8,128)} %get-tuple-element.11.den_ref), custom_call_target="tpu_custom_call" | custom-call | tf_op jit(solution)/shard_map/outer_attention/pallas_call | solution.py:185
  39.4 4.2 %all-to-all-start.2 = ((bf16[4,128,512]{2,1,0:T(8,128)(2,1)}), bf16[4,128,512]{2,1,0:T(8,128)(2,1)S(1)}, u32[]{:S(2)}, u32[]{:S(2)}) async-start(bf16[4,128,512]{2,1,0:T(8,128)(2,1)} %outer_attention.1), calls=%async_computation.2 | async-start | bytes 1048576 | tf_op jit(solution)/shard_map/all_to_all | solution.py:470
  43.8 8.7 %all-to-all-done.2 = bf16[4,128,512]{2,1,0:T(8,128)(2,1)S(1)} async-done(((bf16[4,128,512]{2,1,0:T(8,128)(2,1)}), bf16[4,128,512]{2,1,0:T(8,128)(2,1)S(1)}, u32[]{:S(2)}, u32[]{:S(2)}) %all-to-all-start.2) | async-done | bytes 524320 | tf_op jit(solution)/shard_map/all_to_all | solution.py:470
  52.6 4.8 %fusion.6 = (f32[128]{0:T(128)S(1)}, bf16[128,2048]{1,0:T(8,128)(2,1)S(1)}) fusion(bf16[4,128,512]{2,1,0:T(8,128)(2,1)S(1)} %all-to-all-done.2, bf16[4,512,2048]{2,1,0:T(8,128)(2,1)} %bitcast.57, bf16[128,2048]{1,0:T(8,128)(2,1)S(1)} %copy-done.14), kind=kOutput, calls=%fused_computation.18 | convolution fusion | flops 1075314560 | bytes 9961984 | tf_op jit(solution)/shard_map/gtc,gcd->td/dot_general | solution.py:471
  59.6 6.1 %all-to-all-start.3 = ((bf16[32,16,2048]{2,1,0:T(8,128)(2,1)}), bf16[32,16,2048]{2,1,0:T(8,128)(2,1)}, u32[]{:S(2)}, u32[]{:S(2)}) async-start(bf16[32,16,2048]{2,1,0:T(8,128)(2,1)} %bitcast.59), calls=%async_computation.3 | async-start | bytes 4194304 | tf_op jit(solution)/shard_map/all_to_all | solution.py:485
  70.0 24.2 %all-to-all-done.3.xa.xb = bf16[32,16,2048]{2,1,0:T(8,128)(2,1)} async-done(((bf16[32,16,2048]{2,1,0:T(8,128)(2,1)}), bf16[32,16,2048]{2,1,0:T(8,128)(2,1)}, u32[]{:S(2)}, u32[]{:S(2)}) %all-to-all-start.3) | async-done | bytes 2097184 | tf_op jit(solution)/shard_map/all_to_all | solution.py:485
  94.2 5.4 %all-to-all-start.6 = ((bf16[32,16,2048]{2,1,0:T(8,128)(2,1)}), bf16[32,16,2048]{2,1,0:T(8,128)(2,1)}, u32[]{:S(2)}, u32[]{:S(2)}) async-start(bf16[32,16,2048]{2,1,0:T(8,128)(2,1)} %bitcast.58), calls=%async_computation.6 | async-start | bytes 4194304 | tf_op jit(solution)/shard_map/all_to_all | solution.py:485
  106.9 3.1 fusion.20
  110.1 23.6 %collective-permute-done.1.ua.uf = bf16[352,2048]{1,0:T(8,128)(2,1)S(1)} collective-permute-done((bf16[352,2048]{1,0:T(8,128)(2,1)S(1)}, bf16[352,2048]{1,0:T(8,128)(2,1)S(1)}, u32[]{:S(2)}, u32[]{:S(2)}) %collective-permute-start.1) | collective-permute-done | bytes 1441824 | tf_op jit(solution)/shard_map/ppermute | solution.py:458
  135.4 3.8 %fusion.21 = (bf16[32,8,2048]{2,1,0:T(8,128)(2,1)}, bf16[32,8,2048]{2,1,0:T(8,128)(2,1)}) fusion(bf16[32,16,2048]{2,1,0:T(8,128)(2,1)} %all-to-all-done.6.xa.xb), kind=kLoop, calls=%fused_computation.32 | loop fusion | bytes 4194304 | tf_op jit(solution)/shard_map/slice | solution.py:490
  139.2 27.2 %collective-permute-done.4.ub.uf = bf16[352,2048]{1,0:T(8,128)(2,1)} collective-permute-done((bf16[352,2048]{1,0:T(8,128)(2,1)}, bf16[352,2048]{1,0:T(8,128)(2,1)}, u32[]{:S(2)}, u32[]{:S(2)}) %collective-permute-start.4) | collective-permute-done | bytes 1441824 | tf_op jit(solution)/shard_map/ppermute | solution.py:458
  167.3 30.0 %collective-permute-done.5.db.df = bf16[352,2048]{1,0:T(8,128)(2,1)} collective-permute-done((bf16[352,2048]{1,0:T(8,128)(2,1)}, bf16[352,2048]{1,0:T(8,128)(2,1)}, u32[]{:S(2)}, u32[]{:S(2)}) %collective-permute-start.5) | collective-permute-done | bytes 1441824 | tf_op jit(solution)/shard_map/ppermute | solution.py:458
  197.3 22.5 %collective-permute-done.6.xa = bf16[32,8,2048]{2,1,0:T(8,128)(2,1)} collective-permute-done((bf16[32,8,2048]{2,1,0:T(8,128)(2,1)}, bf16[32,8,2048]{2,1,0:T(8,128)(2,1)}, u32[]{:S(2)}, u32[]{:S(2)}) %collective-permute-start.6) | collective-permute-done | bytes 1048608 | tf_op jit(solution)/shard_map/ppermute | solution.py:491
  219.8 11.7 %pair_ffn.4 = bf16[32,16,2048]{2,1,0:T(8,128)(2,1)} custom-call(bf16[32,8,2048]{2,1,0:T(8,128)(2,1)} %collective-permute-done.6.xa, bf16[32,8,2048]{2,1,0:T(8,128)(2,1)} %collective-permute-done.7.xb, bf16[2,352,2048]{2,1,0:T(8,128)(2,1)} %bitcast.45, bf16[2,352,2048]{2,1,0:T(8,128)(2,1)} %bitcast.51, bf16[2,352,2048]{2,1,0:T(8,128)(2,1)} %d_ref.9, ...), custom_call_target="tpu_custom_call" | custom-call | flops 4429185024 | bytes 21495808 | tf_op jit(solution)/shard_map/pair_ffn/pallas_call | solution.py:352
  231.5 9.3 %all-to-all-start.5 = ((bf16[32,16,2048]{2,1,0:T(8,128)(2,1)}), bf16[32,16,2048]{2,1,0:T(8,128)(2,1)S(1)}, u32[]{:S(2)}, u32[]{:S(2)}) async-start(bf16[32,16,2048]{2,1,0:T(8,128)(2,1)} %pair_ffn.4), calls=%async_computation.5 | async-start | bytes 4194304 | tf_op jit(solution)/shard_map/all_to_all | solution.py:494
  242.2 7.2 %single_ffn.2 = bf16[256,2048]{1,0:T(8,128)(2,1)} custom-call(bf16[32,8,2048]{2,1,0:T(8,128)(2,1)} %collective-permute-done.12.x_ref, bf16[2,352,2048]{2,1,0:T(8,128)(2,1)} %bitcast.46, bf16[2,352,2048]{2,1,0:T(8,128)(2,1)} %bitcast.52, bf16[2,352,2048]{2,1,0:T(8,128)(2,1)} %d_ref.9, bf16[352,2048]{1,0:T(8,128)(2,1)} %collective-permute-done.ga.gf, ...), custom_call_target="tpu_custom_call" | custom-call | flops 2214592512 | bytes 10747904 | tf_op jit(solution)/shard_map/single_ffn/pallas_call | solution.py:287
  251.5 7.2 %single_ffn.3 = bf16[256,2048]{1,0:T(8,128)(2,1)} custom-call(bf16[32,8,2048]{2,1,0:T(8,128)(2,1)} %copy-done.12, bf16[2,352,2048]{2,1,0:T(8,128)(2,1)} %bitcast.47, bf16[2,352,2048]{2,1,0:T(8,128)(2,1)} %bitcast.53, bf16[2,352,2048]{2,1,0:T(8,128)(2,1)} %d_ref.9, bf16[352,2048]{1,0:T(8,128)(2,1)} %copy-done.7, ...), custom_call_target="tpu_custom_call" | custom-call | flops 2214592512 | bytes 10747904 | tf_op jit(solution)/shard_map/single_ffn/pallas_call | solution.py:287
  258.8 11.8 %pair_ffn.5.own = bf16[32,16,2048]{2,1,0:T(8,128)(2,1)} custom-call(bf16[32,16,2048]{2,1,0:T(8,128)(2,1)} %all-to-all-done.6.xa.xb, bf16[32,16,2048]{2,1,0:T(8,128)(2,1)} %all-to-all-done.6.xa.xb, bf16[2,352,2048]{2,1,0:T(8,128)(2,1)} %bitcast.48, bf16[2,352,2048]{2,1,0:T(8,128)(2,1)} %bitcast.54, bf16[2,352,2048]{2,1,0:T(8,128)(2,1)} %d_ref.9, ...), custom_call_target="tpu_custom_call" | custom-call | flops 4429185024 | bytes 21495808 | tf_op jit(solution)/shard_map/pair_ffn/pallas_call | solution.py:352
  270.6 3.8 %collective-permute-done.13.came_a = bf16[256,2048]{1,0:T(8,128)(2,1)S(1)} collective-permute-done((bf16[256,2048]{1,0:T(8,128)(2,1)}, bf16[256,2048]{1,0:T(8,128)(2,1)S(1)}, u32[]{:S(2)}, u32[]{:S(2)}) %collective-permute-start.13) | collective-permute-done | bytes 1048608 | tf_op jit(solution)/shard_map/ppermute | solution.py:516
  274.4 7.8 %collective-permute-done.15.came_b = bf16[256,2048]{1,0:T(8,128)(2,1)S(1)} collective-permute-done((bf16[256,2048]{1,0:T(8,128)(2,1)}, bf16[256,2048]{1,0:T(8,128)(2,1)S(1)}, u32[]{:S(2)}, u32[]{:S(2)}) %collective-permute-start.15) | collective-permute-done | bytes 1048608 | tf_op jit(solution)/shard_map/ppermute | solution.py:516
  285.7 9.6 %all-to-all-start.7 = ((bf16[32,16,2048]{2,1,0:T(8,128)(2,1)}), bf16[32,16,2048]{2,1,0:T(8,128)(2,1)}, u32[]{:S(2)}, u32[]{:S(2)}) async-start(bf16[32,16,2048]{2,1,0:T(8,128)(2,1)} %merge.1), calls=%async_computation.7 | async-start | bytes 4194304 | tf_op jit(solution)/shard_map/all_to_all | solution.py:494
  295.4 11.8 %pair_ffn.3 = bf16[32,16,2048]{2,1,0:T(8,128)(2,1)} custom-call(bf16[32,16,2048]{2,1,0:T(8,128)(2,1)} %all-to-all-done.3.xa.xb, bf16[32,16,2048]{2,1,0:T(8,128)(2,1)} %all-to-all-done.3.xa.xb, bf16[2,352,2048]{2,1,0:T(8,128)(2,1)} %bitcast.49, bf16[2,352,2048]{2,1,0:T(8,128)(2,1)} %bitcast.55, bf16[2,352,2048]{2,1,0:T(8,128)(2,1)} %d_ref.9, ...), custom_call_target="tpu_custom_call" | custom-call | flops 4429185024 | bytes 21495808 | tf_op jit(solution)/shard_map/pair_ffn/pallas_call | solution.py:352
  307.2 16.6 %all-to-all-done.7 = bf16[32,16,2048]{2,1,0:T(8,128)(2,1)} async-done(((bf16[32,16,2048]{2,1,0:T(8,128)(2,1)}), bf16[32,16,2048]{2,1,0:T(8,128)(2,1)}, u32[]{:S(2)}, u32[]{:S(2)}) %all-to-all-start.7) | async-done | bytes 2097184 | tf_op jit(solution)/shard_map/all_to_all | solution.py:494
  323.8 5.2 %all-to-all-start.4 = ((bf16[32,16,2048]{2,1,0:T(8,128)(2,1)}), bf16[32,16,2048]{2,1,0:T(8,128)(2,1)}, u32[]{:S(2)}, u32[]{:S(2)}) async-start(bf16[32,16,2048]{2,1,0:T(8,128)(2,1)} %pair_ffn.3), calls=%async_computation.4 | async-start | bytes 4194304 | tf_op jit(solution)/shard_map/all_to_all | solution.py:494
  330.8 3.0 collective-permute-done.8.mix_a
  338.9 18.5 %all-to-all-done.4 = bf16[32,16,2048]{2,1,0:T(8,128)(2,1)} async-done(((bf16[32,16,2048]{2,1,0:T(8,128)(2,1)}), bf16[32,16,2048]{2,1,0:T(8,128)(2,1)}, u32[]{:S(2)}, u32[]{:S(2)}) %all-to-all-start.4) | async-done | bytes 2097184 | tf_op jit(solution)/shard_map/all_to_all | solution.py:494
  357.4 3.1 fusion.5
  (70 shorter events, 32.4 us)
Async XLA Ops:
  22.6 12.2 %all-to-all-start.1 = ((bf16[32,24,128]{2,1,0:T(8,128)(2,1)}), bf16[32,24,128]{2,1,0:T(8,128)(2,1)S(1)}, u32[]{:S(2)}, u32[]{:S(2)}) async-start(bf16[32,24,128]{2,1,0:T(8,128)(2,1)} %prior_states.1), calls=%async_computation.1 | async-start | bytes 393216 | tf_op jit(solution)/shard_map/all_to_all | solution.py:467
  32.0 11.6 %copy-start.1 = (s32[128,6]{0,1:T(8,128)S(1)}, s32[128,6]{0,1:T(8,128)}, u32[]{:S(2)}) copy-start(s32[128,6]{0,1:T(8,128)} %param.19) | copy-start | bytes 9220
  32.0 11.6 %copy-start.2 = (f32[128,6]{0,1:T(8,128)S(1)}, f32[128,6]{0,1:T(8,128)}, u32[]{:S(2)}) copy-start(f32[128,6]{0,1:T(8,128)} %param.20) | copy-start | bytes 9220
  32.0 20.5 %copy-start.14 = (bf16[128,2048]{1,0:T(8,128)(2,1)S(1)}, bf16[128,2048]{1,0:T(8,128)(2,1)}, u32[]{:S(2)}) copy-start(bf16[128,2048]{1,0:T(8,128)(2,1)} %param.16) | copy-start | bytes 1572868
  39.4 13.2 %all-to-all-start.2 = ((bf16[4,128,512]{2,1,0:T(8,128)(2,1)}), bf16[4,128,512]{2,1,0:T(8,128)(2,1)S(1)}, u32[]{:S(2)}, u32[]{:S(2)}) async-start(bf16[4,128,512]{2,1,0:T(8,128)(2,1)} %outer_attention.1), calls=%async_computation.2 | async-start | bytes 1048576 | tf_op jit(solution)/shard_map/all_to_all | solution.py:470
  52.6 4.9 %copy-start.15 = (f32[2048]{0:T(1024)S(1)}, f32[2048]{0:T(1024)}, u32[]{:S(2)}) copy-start(f32[2048]{0:T(1024)} %param.18) | copy-start | bytes 24580
  59.6 6.1 %copy-start.3 = (bf16[2,2048,352]{1,2,0:T(8,128)(2,1)S(1)}, bf16[2,2048,352]{1,2,0:T(8,128)(2,1)}, u32[]{:S(2)}) copy-start(bf16[2,2048,352]{1,2,0:T(8,128)(2,1)} %param.21) | copy-start | bytes 8650756
  59.6 34.5 %all-to-all-start.3 = ((bf16[32,16,2048]{2,1,0:T(8,128)(2,1)}), bf16[32,16,2048]{2,1,0:T(8,128)(2,1)}, u32[]{:S(2)}, u32[]{:S(2)}) async-start(bf16[32,16,2048]{2,1,0:T(8,128)(2,1)} %bitcast.59), calls=%async_computation.3 | async-start | bytes 4194304 | tf_op jit(solution)/shard_map/all_to_all | solution.py:485
  67.6 38.5 %collective-permute-start = (bf16[352,2048]{1,0:T(8,128)(2,1)}, bf16[352,2048]{1,0:T(8,128)(2,1)}, u32[]{:S(2)}, u32[]{:S(2)}) collective-permute-start(bf16[352,2048]{1,0:T(8,128)(2,1)} %get-tuple-element.23), channel_id=1, source_target_pairs={{0,1},{1,0},{2,3},{3,2},{4,5},{5,4},{6,7},{7,6},{8,9},{9,8},{10,11... | collective-permute-start | bytes 4325384 | tf_op jit(solution)/shard_map/ppermute | solution.py:458
  94.2 5.5 %copy-start.4 = (bf16[2,2048,352]{1,2,0:T(8,128)(2,1)S(1)}, bf16[2,2048,352]{1,2,0:T(8,128)(2,1)}, u32[]{:S(2)}) copy-start(bf16[2,2048,352]{1,2,0:T(8,128)(2,1)} %param.22) | copy-start | bytes 8650756
  94.2 41.2 %all-to-all-start.6 = ((bf16[32,16,2048]{2,1,0:T(8,128)(2,1)}), bf16[32,16,2048]{2,1,0:T(8,128)(2,1)}, u32[]{:S(2)}, u32[]{:S(2)}) async-start(bf16[32,16,2048]{2,1,0:T(8,128)(2,1)} %bitcast.58), calls=%async_computation.6 | async-start | bytes 4194304 | tf_op jit(solution)/shard_map/all_to_all | solution.py:485
  99.6 4.5 %copy-start.5 = (bf16[2,352,2048]{2,1,0:T(8,128)(2,1)S(1)}, bf16[2,352,2048]{2,1,0:T(8,128)(2,1)}, u32[]{:S(2)}) copy-start(bf16[2,352,2048]{2,1,0:T(8,128)(2,1)} %d_ref.9) | copy-start | bytes 8650756
  101.0 32.7 %collective-permute-start.1 = (bf16[352,2048]{1,0:T(8,128)(2,1)S(1)}, bf16[352,2048]{1,0:T(8,128)(2,1)S(1)}, u32[]{:S(2)}, u32[]{:S(2)}) collective-permute-start(bf16[352,2048]{1,0:T(8,128)(2,1)S(1)} %get-tuple-element.21), channel_id=1, source_target_pairs={{0,1},{1,0},{2,3},{3,2},{4,5},{5,4},{6,7},{7,6},{8,9},{9,8},{10,11... | collective-permute-start | bytes 4325384 | tf_op jit(solution)/shard_map/ppermute | solution.py:458
  101.5 33.9 %collective-permute-start.3 = (bf16[352,2048]{1,0:T(8,128)(2,1)S(1)}, bf16[352,2048]{1,0:T(8,128)(2,1)S(1)}, u32[]{:S(2)}, u32[]{:S(2)}) collective-permute-start(bf16[352,2048]{1,0:T(8,128)(2,1)S(1)} %copy-done.11), channel_id=1, source_target_pairs={{0,3},{3,0},{1,2},{2,1},{4,7},{7,4},{5,6},{6,5},{8,11},{11,8},{9,1... | collective-permute-start | bytes 4325384 | tf_op jit(solution)/shard_map/ppermute | solution.py:458
  102.4 64.0 %collective-permute-start.4 = (bf16[352,2048]{1,0:T(8,128)(2,1)}, bf16[352,2048]{1,0:T(8,128)(2,1)}, u32[]{:S(2)}, u32[]{:S(2)}) collective-permute-start(bf16[352,2048]{1,0:T(8,128)(2,1)} %get-tuple-element.20), channel_id=1, source_target_pairs={{0,3},{3,0},{1,2},{2,1},{4,7},{7,4},{5,6},{6,5},{8,11},{11,8},{9,1... | collective-permute-start | bytes 4325384 | tf_op jit(solution)/shard_map/ppermute | solution.py:458
  106.0 61.3 %collective-permute-start.2 = (bf16[352,2048]{1,0:T(8,128)(2,1)}, bf16[352,2048]{1,0:T(8,128)(2,1)}, u32[]{:S(2)}, u32[]{:S(2)}) collective-permute-start(bf16[352,2048]{1,0:T(8,128)(2,1)} %get-tuple-element.19), channel_id=1, source_target_pairs={{0,1},{1,0},{2,3},{3,2},{4,5},{5,4},{6,7},{7,6},{8,9},{9,8},{10,11... | collective-permute-start | bytes 4325384 | tf_op jit(solution)/shard_map/ppermute | solution.py:458
  106.1 91.2 %collective-permute-start.5 = (bf16[352,2048]{1,0:T(8,128)(2,1)}, bf16[352,2048]{1,0:T(8,128)(2,1)}, u32[]{:S(2)}, u32[]{:S(2)}) collective-permute-start(bf16[352,2048]{1,0:T(8,128)(2,1)} %get-tuple-element.18), channel_id=1, source_target_pairs={{0,3},{3,0},{1,2},{2,1},{4,7},{7,4},{5,6},{6,5},{8,11},{11,8},{9,1... | collective-permute-start | bytes 4325384 | tf_op jit(solution)/shard_map/ppermute | solution.py:458
  133.7 5.5 %copy-start.6 = (bf16[352,2048]{1,0:T(8,128)(2,1)}, bf16[352,2048]{1,0:T(8,128)(2,1)S(1)}, u32[]{:S(2)}) copy-start(bf16[352,2048]{1,0:T(8,128)(2,1)S(1)} %collective-permute-done.1.ua.uf) | copy-start | bytes 4325380
  133.7 86.1 %collective-permute-start.6 = (bf16[32,8,2048]{2,1,0:T(8,128)(2,1)}, bf16[32,8,2048]{2,1,0:T(8,128)(2,1)}, u32[]{:S(2)}, u32[]{:S(2)}) collective-permute-start(bf16[32,8,2048]{2,1,0:T(8,128)(2,1)} %get-tuple-element.25), channel_id=1, source_target_pairs={{0,3},{3,0},{1,2},{2,1},{4,7},{7,4},{5,6},{6,5},{8,11},{11,8},{9,1... | collective-permute-start | bytes 3145736 | tf_op jit(solution)/shard_map/ppermute | solution.py:491
  135.4 84.4 %collective-permute-start.7 = (bf16[32,8,2048]{2,1,0:T(8,128)(2,1)}, bf16[32,8,2048]{2,1,0:T(8,128)(2,1)}, u32[]{:S(2)}, u32[]{:S(2)}) collective-permute-start(bf16[32,8,2048]{2,1,0:T(8,128)(2,1)} %get-tuple-element.24), channel_id=1, source_target_pairs={{0,1},{1,0},{2,3},{3,2},{4,5},{5,4},{6,7},{7,6},{8,9},{9,8},{10,11... | collective-permute-start | bytes 3145736 | tf_op jit(solution)/shard_map/ppermute | solution.py:491
  166.4 75.8 %collective-permute-start.12 = (bf16[32,8,2048]{2,1,0:T(8,128)(2,1)}, bf16[32,8,2048]{2,1,0:T(8,128)(2,1)}, u32[]{:S(2)}, u32[]{:S(2)}) collective-permute-start(bf16[32,8,2048]{2,1,0:T(8,128)(2,1)} %get-tuple-element.27), channel_id=1, source_target_pairs={{0,3},{3,0},{1,2},{2,1},{4,7},{7,4},{5,6},{6,5},{8,11},{11,8},{9,1... | collective-permute-start | bytes 3145736 | tf_op jit(solution)/shard_map/ppermute | solution.py:491
  167.3 83.1 %collective-permute-start.14 = (bf16[32,8,2048]{2,1,0:T(8,128)(2,1)}, bf16[32,8,2048]{2,1,0:T(8,128)(2,1)S(1)}, u32[]{:S(2)}, u32[]{:S(2)}) collective-permute-start(bf16[32,8,2048]{2,1,0:T(8,128)(2,1)} %get-tuple-element.26), channel_id=1, source_target_pairs={{0,1},{1,0},{2,3},{3,2},{4,5},{5,4},{6,7},{7,6},{8,9},{9,8},{10,11... | collective-permute-start | bytes 3145736 | tf_op jit(solution)/shard_map/ppermute | solution.py:491
  231.5 54.2 %all-to-all-start.5 = ((bf16[32,16,2048]{2,1,0:T(8,128)(2,1)}), bf16[32,16,2048]{2,1,0:T(8,128)(2,1)S(1)}, u32[]{:S(2)}, u32[]{:S(2)}) async-start(bf16[32,16,2048]{2,1,0:T(8,128)(2,1)} %pair_ffn.4), calls=%async_computation.5 | async-start | bytes 4194304 | tf_op jit(solution)/shard_map/all_to_all | solution.py:494
  249.4 24.9 %collective-permute-start.13 = (bf16[256,2048]{1,0:T(8,128)(2,1)}, bf16[256,2048]{1,0:T(8,128)(2,1)S(1)}, u32[]{:S(2)}, u32[]{:S(2)}) collective-permute-start(bf16[256,2048]{1,0:T(8,128)(2,1)} %single_ffn.2), channel_id=1, source_target_pairs={{0,3},{3,0},{1,2},{2,1},{4,7},{7,4},{5,6},{6,5},{8,11},{11,8},{9,1... | collective-permute-start | bytes 3145736 | tf_op jit(solution)/shard_map/ppermute | solution.py:516
  258.7 23.4 %collective-permute-start.15 = (bf16[256,2048]{1,0:T(8,128)(2,1)}, bf16[256,2048]{1,0:T(8,128)(2,1)S(1)}, u32[]{:S(2)}, u32[]{:S(2)}) collective-permute-start(bf16[256,2048]{1,0:T(8,128)(2,1)} %single_ffn.3), channel_id=1, source_target_pairs={{0,1},{1,0},{2,3},{3,2},{4,5},{5,4},{6,7},{7,6},{8,9},{9,8},{10,11... | collective-permute-start | bytes 3145736 | tf_op jit(solution)/shard_map/ppermute | solution.py:516
  285.7 38.0 %all-to-all-start.7 = ((bf16[32,16,2048]{2,1,0:T(8,128)(2,1)}), bf16[32,16,2048]{2,1,0:T(8,128)(2,1)}, u32[]{:S(2)}, u32[]{:S(2)}) async-start(bf16[32,16,2048]{2,1,0:T(8,128)(2,1)} %merge.1), calls=%async_computation.7 | async-start | bytes 4194304 | tf_op jit(solution)/shard_map/all_to_all | solution.py:494
  323.8 33.7 %all-to-all-start.4 = ((bf16[32,16,2048]{2,1,0:T(8,128)(2,1)}), bf16[32,16,2048]{2,1,0:T(8,128)(2,1)}, u32[]{:S(2)}, u32[]{:S(2)}) async-start(bf16[32,16,2048]{2,1,0:T(8,128)(2,1)} %pair_ffn.3), calls=%async_computation.4 | async-start | bytes 4194304 | tf_op jit(solution)/shard_map/all_to_all | solution.py:494
  328.9 4.8 %collective-permute-start.8 = (bf16[256,128]{1,0:T(8,128)(2,1)S(1)}, bf16[256,128]{1,0:T(8,128)(2,1)S(1)}, u32[]{:S(2)}, u32[]{:S(2)}) collective-permute-start(bf16[256,128]{1,0:T(8,128)(2,1)S(1)} %get-tuple-element.14), channel_id=1, source_target_pairs={{0,3},{3,0},{1,2},{2,1},{4,7},{7,4},{5,6},{6,5},{8,11},{11,8},{9,1... | collective-permute-start | bytes 196616 | tf_op jit(solution)/shard_map/ppermute | solution.py:464
  330.8 3.5 collective-permute-start.9
  335.6 21.9 %copy-start.10 = (bf16[128,2048]{1,0:T(8,128)(2,1)S(1)}, bf16[128,2048]{1,0:T(8,128)(2,1)}, u32[]{:S(2)}) copy-start(bf16[128,2048]{1,0:T(8,128)(2,1)} %copy-done.8) | copy-start | bytes 1572868
  335.6 21.8 %collective-permute-start.10 = (bf16[128,2048]{1,0:T(8,128)(2,1)S(1)}, bf16[128,2048]{1,0:T(8,128)(2,1)S(1)}, u32[]{:S(2)}, u32[]{:S(2)}) collective-permute-start(bf16[128,2048]{1,0:T(8,128)(2,1)S(1)} %get-tuple-element.16), channel_id=1, source_target_pairs={{0,3},{3,0},{1,2},{2,1},{4,7},{7,4},{5,6},{6,5},{8,11},{11,8},{9,1... | collective-permute-start | bytes 1572872 | tf_op jit(solution)/shard_map/ppermute | solution.py:509
  336.9 20.6 %collective-permute-start.11 = (bf16[128,2048]{1,0:T(8,128)(2,1)S(1)}, bf16[128,2048]{1,0:T(8,128)(2,1)}, u32[]{:S(2)}, u32[]{:S(2)}) collective-permute-start(bf16[128,2048]{1,0:T(8,128)(2,1)S(1)} %get-tuple-element.17), channel_id=1, source_target_pairs={{0,1},{1,0},{2,3},{3,2},{4,5},{5,4},{6,7},{7,6},{8,9},{9,8},{10,11... | collective-permute-start | bytes 1572872 | tf_op jit(solution)/shard_map/ppermute | solution.py:510
  (7 other events, 13.3 us)
where the time goes:
time: 362 us; the launch traced here: 361 us
  waiting for transfers between devices  191 us (53%)
  Pallas kernels  67 us (19%)
  starting transfers between devices  53.8 us (15%)
  blocking collectives  17.7 us (5%)
  local copies, waits for them, and re-layouts  15.5 us (4%)
  matrix products  14.3 us (4%)
    ppermute x6, waiting for transfers between devices, on_device(): far_w[which].append(lax.ppermute(w[which], 'grp', pairs[which][0]))  81.6 us
    pallas_call x3, Pallas kernels, pair_ffn(): pl.pallas_call(functools.partial(pair_body, starts), out_shape=jax.ShapeD...  35.3 us
    all_to_all x3, waiting for transfers between devices, home(): return lax.all_to_all(rows, 'ctx', 0, 0, tiled=True)  35.1 us
    all_to_all x2, waiting for transfers between devices, on_device(): lax.all_to_all(buffer.reshape(n_ctx, 2 * half, D), 'ctx', 0, 0, tiled=True)  24.2 us
    all_to_all x3, starting transfers between devices, home(): return lax.all_to_all(rows, 'ctx', 0, 0, tiled=True)  24.1 us
    ppermute x4, waiting for transfers between devices, on_device(): others.append(lax.ppermute(own, 'grp', pairs[which][1]))  23.9 us
    all_to_all x1, blocking collectives, on_device(): got = lax.all_to_all(payload, 'ctx', 0, 0, tiled=True)  17.7 us
    pallas_call x2, Pallas kernels, single_ffn(): pl.pallas_call(functools.partial(single_body, which), out_shape=jax.Shape...  14.4 us
  transfers between devices with their start and end apart: 23, of which 15 were waited for; matrix products, arithmetic and copies ran while one was open for 4% of the time, Pallas kernels for 16%

commit v1 on v0

--- a/solution.py
+++ b/solution.py
@@ -16,6 +16,7 @@
 CHUNKS = 2
 EXTRA = 8
 GRANT = 58 << 20
+KEEP_GRANT = 24 << 20
 FAR = [(0, 3), (3, 0), (1, 2), (2, 1)]
 NEAR = [(0, 1), (1, 0), (2, 3), (3, 2)]
 F32 = jnp.float32
@@ -74,7 +75,7 @@
     return pl.pallas_call(
         state_body,
         out_shape=jax.ShapeDtypeStruct((blocks, SLOTS + EXTRA, HD), BF16),
-        compiler_params=pltpu.CompilerParams(vmem_limit_bytes=GRANT),
+        compiler_params=pltpu.CompilerParams(vmem_limit_bytes=8 << 20),
         name="local_states",
     )(keys, values, decay)
 
@@ -230,143 +231,136 @@
     )(ids, gates)
 
 
-def contract_last(x, y):
-    return lax.dot_general(x, y, (((1,), (1,)), ((), ())), preferred_element_type=F32)
-
-
-def apply_half(x, weights, store, waits):
-    waits(0)
-    gate = contract_last(x, weights[0])
-    waits(1)
-    up = contract_last(x, weights[1])
+NT = (((1,), (1,)), ((), ()))
+TN = (((0,), (0,)), ((), ()))
+
+
+def expert_rows(x, weights, e, ready, emit):
+    ready(0)
+    gate = lax.dot_general(weights[e, 0], x, NT, preferred_element_type=F32)
+    ready(1)
+    up = lax.dot_general(weights[e, 1], x, NT, preferred_element_type=F32)
     hidden = (jax.nn.silu(gate) * up).astype(BF16)
-    waits(2)
+    ready(2)
     width = D // 4
 
-    def down(i, carry):
-        at = pl.multiple_of(i * width, width)
-        store(at, width, jnp.dot(hidden, weights[2, :, pl.ds(at, width)], preferred_element_type=F32))
+    def down(i, inner):
+        cols = pl.ds(pl.multiple_of(i * width, width), width)
+        part = lax.dot_general(hidden, weights[e, 2, :, cols], TN, preferred_element_type=F32)
+        emit(cols, part.astype(BF16))
+        return inner
+
+    lax.fori_loop(0, 4, down, 0)
+
+
+def experts_body(sets, *refs):
+    count = 1 + max(at for pair in sets for at, _ in pair)
+    rows_in = refs[:count]
+    own = refs[count : count + 3]
+    fars = (refs[count + 3 : count + 6], refs[count + 6 : count + 9])
+    outs = refs[count + 9 : count + 9 + len(sets)]
+    ws, xs, sems = refs[-3:]
+    quarter = fars[0][0].shape[0]
+    _, n_sets, blocks, rows, _ = xs.shape
+    for e in range(2):
+        for j, pair in enumerate(sets):
+            at, first = pair[e]
+            source = rows_in[at].at[:, first : first + rows, :]
+            pltpu.make_async_copy(source, xs.at[e, j], sems.at[e, 6 + j]).start()
+        for i in range(3):
+            low = ws.at[e, i, 0:quarter]
+            high = ws.at[e, i, quarter : 2 * quarter]
+            pltpu.make_async_copy(own[i].at[e], low, sems.at[e, 2 * i]).start()
+            pltpu.make_async_copy(fars[e][i], high, sems.at[e, 2 * i + 1]).start()
+
+    def expert(e, carry):
+        def ready(i):
+            for part in range(2):
+                held = ws.at[e, i, part * quarter : (part + 1) * quarter]
+                pltpu.make_async_copy(fars[0][0], held, sems.at[e, 2 * i + part]).wait()
+
+        def emit(cols, part):
+            at = pl.ds(pl.multiple_of(e * rows, rows), rows)
+            part = part.reshape(n_sets, blocks, rows, part.shape[1])
+            for j in range(n_sets):
+                outs[j][:, at, cols] = part[j]
+
+        for j in range(n_sets):
+            pltpu.make_async_copy(
+                rows_in[0].at[:, 0:rows, :], xs.at[e, j], sems.at[e, 6 + j]
+            ).wait()
+        expert_rows(xs[e].reshape(-1, D), ws, e, ready, emit)
         return carry
 
-    lax.fori_loop(0, 4, down, 0)
-
-
-def single_body(which, x_ref, g_ref, u_ref, d_ref, gf, uf, df, out_ref, xs, ws, sems):
-    quarter = gf.shape[0]
-    copies = []
-    for i, (own, far) in enumerate(((g_ref, gf), (u_ref, uf), (d_ref, df))):
-        copies.append(
-            (
-                pltpu.make_async_copy(own.at[which], ws.at[i, 0:quarter], sems.at[2 * i]),
-                pltpu.make_async_copy(far, ws.at[i, quarter : 2 * quarter], sems.at[2 * i + 1]),
-            )
-        )
-    x_copy = pltpu.make_async_copy(x_ref, xs, sems.at[6])
-    x_copy.start()
-    for pair in copies:
-        for copy in pair:
-            copy.start()
-    x_copy.wait()
-
-    def waits(i):
-        for copy in copies[i]:
-            copy.wait()
-
-    def store(at, width, value):
-        out_ref[:, pl.ds(at, width)] = value.astype(BF16)
-
-    apply_half(xs[...].reshape(-1, D), ws, store, waits)
-
-
-def single_ffn(x, own, far, which):
-    quarter = far[0].shape[0]
-    blocks, rows, _ = x.shape
-    total = blocks * rows
+    lax.fori_loop(0, 2, expert, 0)
+
+
+def expert_cost(total, quarter, loaded):
+    return pl.CostEstimate(
+        flops=12 * total * quarter * D,
+        bytes_accessed=loaded * 24 * quarter * D + 4 * total * D,
+        transcendentals=2 * total * quarter,
+    )
+
+
+def experts(xs, sets, own, fars, keep=False):
+    quarter = fars[0][0].shape[0]
+    blocks = xs[0].shape[0]
+    rows = SLOTS // CHUNKS
+    out_shape = [jax.ShapeDtypeStruct((blocks, 2 * rows, D), BF16)] * len(sets)
     anywhere = pl.BlockSpec(memory_space=pl.ANY)
-    held = pl.BlockSpec(memory_space=pltpu.HBM)
-    return pl.pallas_call(
-        functools.partial(single_body, which),
-        out_shape=jax.ShapeDtypeStruct((total, D), BF16),
-        in_specs=[anywhere] + [held] * 6,
-        out_specs=pl.BlockSpec(memory_space=pltpu.VMEM),
-        scratch_shapes=[
-            pltpu.VMEM((blocks, rows, D), BF16),
-            pltpu.VMEM((3, 2 * quarter, D), BF16),
-            pltpu.SemaphoreType.DMA((7,)),
-        ],
-        compiler_params=pltpu.CompilerParams(vmem_limit_bytes=GRANT),
-        cost_estimate=pl.CostEstimate(
-            flops=12 * total * quarter * D,
-            bytes_accessed=12 * quarter * D + 4 * total * D,
-            transcendentals=2 * total * quarter,
-        ),
-        name="single_ffn",
-    )(x, *own, *far)
-
-
-def pair_body(starts, xa, xb, g_ref, u_ref, d_ref, ga, ua, da, gb, ub, db, out_ref, xs, ws, sems):
-    quarter = ga.shape[0]
-    blocks, rows, _ = out_ref.shape
-    rows = rows // 2
-    for e, (x_ref, fars) in enumerate(((xa, (ga, ua, da)), (xb, (gb, ub, db)))):
-        pltpu.make_async_copy(
-            x_ref.at[:, starts[e] : starts[e] + rows, :], xs.at[e], sems.at[7 * e + 6]
-        ).start()
-        for i, (own, far) in enumerate(zip((g_ref, u_ref, d_ref), fars)):
-            pair = (
-                pltpu.make_async_copy(own.at[e], ws.at[e, i, 0:quarter], sems.at[7 * e + 2 * i]),
-                pltpu.make_async_copy(
-                    far, ws.at[e, i, quarter : 2 * quarter], sems.at[7 * e + 2 * i + 1]
-                ),
-            )
-            for copy in pair:
-                copy.start()
+    held = pltpu.VMEM((2, 3, 2 * quarter, D), BF16)
+    scratch = [
+        pltpu.VMEM((2, len(sets), blocks, rows, D), BF16),
+        pltpu.SemaphoreType.DMA((2, 6 + len(sets))),
+    ]
+    return pl.pallas_call(
+        functools.partial(experts_body, sets),
+        out_shape=out_shape + [held] if keep else out_shape,
+        in_specs=[anywhere] * (len(xs) + 9),
+        scratch_shapes=scratch if keep else [held] + scratch,
+        compiler_params=pltpu.CompilerParams(vmem_limit_bytes=KEEP_GRANT if keep else GRANT),
+        cost_estimate=expert_cost(2 * blocks * rows * len(sets), quarter, 1),
+        name="experts",
+    )(*xs, *own, *fars[0], *fars[1])
+
+
+def last_body(xa, xb, weights, out_a, out_b, xs, sems):
+    outs = (out_a, out_b)
+    for e, x_ref in enumerate((xa, xb)):
+        pltpu.make_async_copy(x_ref, xs.at[e], sems.at[e]).start()
 
     def expert(e, carry):
-        def wait_for(ref, dst, sem):
-            pltpu.make_async_copy(ref, dst, sems.at[7 * e + sem]).wait()
-
-        wait_for(xa.at[:, 0:rows, :], xs.at[e], 6)
-
-        def waits(i):
-            wait_for(ga, ws.at[e, i, 0:quarter], 2 * i)
-            wait_for(ga, ws.at[e, i, quarter : 2 * quarter], 2 * i + 1)
-
-        def store(at, width, value):
-            where = pl.ds(pl.multiple_of(e * rows, rows), rows)
-            out_ref[:, where, pl.ds(at, width)] = value.astype(BF16).reshape(blocks, rows, width)
-
-        apply_half(xs[e].reshape(-1, D), ws.at[e], store, waits)
+        def emit(cols, part):
+            for k in range(2):
+
+                @pl.when(e == k)
+                def _():
+                    outs[k][:, cols] = part
+
+        pltpu.make_async_copy(xa, xs.at[e], sems.at[e]).wait()
+        expert_rows(xs[e].reshape(-1, D), weights, e, lambda i: None, emit)
         return carry
 
     lax.fori_loop(0, 2, expert, 0)
 
 
-def pair_ffn(xa, xb, starts, own, fars):
-    quarter = fars[0][0].shape[0]
-    blocks = xa.shape[0]
-    rows = SLOTS // CHUNKS
-    total = 2 * blocks * rows
+def last_experts(xa, xb, weights):
+    blocks, rows, _ = xa.shape
     anywhere = pl.BlockSpec(memory_space=pl.ANY)
-    held = pl.BlockSpec(memory_space=pltpu.HBM)
-    return pl.pallas_call(
-        functools.partial(pair_body, starts),
-        out_shape=jax.ShapeDtypeStruct((blocks, 2 * rows, D), BF16),
-        in_specs=[anywhere] * 2 + [held] * 9,
-        out_specs=pl.BlockSpec(memory_space=pltpu.VMEM),
+    on_chip = pl.BlockSpec(memory_space=pltpu.VMEM)
+    return pl.pallas_call(
+        last_body,
+        out_shape=[jax.ShapeDtypeStruct((blocks * rows, D), BF16)] * 2,
+        in_specs=[anywhere, anywhere, on_chip],
         scratch_shapes=[
             pltpu.VMEM((2, blocks, rows, D), BF16),
-            pltpu.VMEM((2, 3, 2 * quarter, D), BF16),
-            pltpu.SemaphoreType.DMA((14,)),
+            pltpu.SemaphoreType.DMA((2,)),
         ],
-        compiler_params=pltpu.CompilerParams(vmem_limit_bytes=GRANT),
-        cost_estimate=pl.CostEstimate(
-            flops=12 * total * quarter * D,
-            bytes_accessed=24 * quarter * D + 4 * total * D,
-            transcendentals=2 * total * quarter,
-        ),
-        name="pair_ffn",
-    )(xa, xb, *own, *fars[0], *fars[1])
+        compiler_params=pltpu.CompilerParams(vmem_limit_bytes=KEEP_GRANT),
+        cost_estimate=expert_cost(2 * blocks * rows, weights.shape[2] // 2, 0),
+        name="last_experts",
+    )(xa, xb, weights)
 
 
 def merge_body(own, came_a, came_b, out):
@@ -501,22 +495,27 @@
             preferred_element_type=F32,
         )
 
-    own0 = pair_ffn(sent[0], sent[0], (0, half), own_w, far_w)
+    (own0,) = experts((sent[0],), (((0, 0), (0, half)),), own_w, far_w)
     back_own0 = home(own0)
-    other0 = pair_ffn(others[0], others[1], (0, 0), own_w, far_w)
+    own1, other0, held = experts(
+        (sent[1], others[0], others[1]),
+        (((0, 0), (0, half)), ((1, 0), (2, 0))),
+        own_w,
+        far_w,
+        keep=True,
+    )
     back_other0 = home(other0)
     for_far, for_near = partner_mix(back_other0, far_even, near_odd)
     from_far = lax.ppermute(for_far, "grp", FAR)
     from_near = lax.ppermute(for_near, "grp", NEAR)
 
-    own1 = pair_ffn(sent[1], sent[1], (0, half), own_w, far_w)
+    results = last_experts(others[2], others[3], held)
     came = []
     for which in range(2):
-        other = single_ffn(others[2 + which], own_w, far_w[which], which)
-        came.append(lax.ppermute(other, "grp", pairs[which][1]))
+        came.append(lax.ppermute(results[which], "grp", pairs[which][1]))
     back1 = home(merge(own1, *came))
-    total = widened + mix(0, back_own0) + from_far.astype(F32) + from_near.astype(F32)
-    total = total + mix(1, back1)
+    so_far = lax.optimization_barrier(widened + mix(0, back_own0))
+    total = so_far + from_far.astype(F32) + from_near.astype(F32) + mix(1, back1)
     return (attended, total.astype(BF16))
 
 

time: 362 us -> 332 us (0.917)
  waiting for transfers between devices: 191 us -> 160 us
  Pallas kernels: 67 us -> 51 us
  local copies, waits for them, and re-layouts: 15.5 us -> 29.8 us
  starting transfers between devices: 53.8 us -> 58.2 us
    all_to_all x3, waiting for transfers between devices: 35.1 us -> 8.75 us  [home(): return lax.all_to_all(rows, 'ctx', 0, 0, tiled=True)]
    ppermute x6, waiting for transfers between devices: 81.6 us -> 63.7 us  [on_device(): far_w[which].append(lax.ppermute(w[which], 'grp', pairs[which][0]))]
    unnamed x32 -> x48, local copies, waits for them, and re-layouts: 3.58 us -> 18.9 us
    pallas_call x5 -> x3, Pallas kernels: 49.7 us -> 35.5 us  [the longest x2 28.6 us: experts(): pl.pallas_call(functools.partial(experts_body, sets), out_shape=out_shape...]
    ppermute x2, waiting for transfers between devices: 11.6 us -> 24.2 us  [on_device(): came.append(lax.ppermute(results[which], 'grp', pairs[which][1]))]
    ppermute x1, waiting for transfers between devices: 0.01 us -> 10.5 us  [on_device(): from_far = lax.ppermute(for_far, 'grp', FAR)]
    all_to_all x2, waiting for transfers between devices: 24.2 us -> 18.5 us  [on_device(): lax.all_to_all(buffer.reshape(n_ctx, 2 * half, D), 'ctx', 0, 0, tiled=True)]
    ppermute x4, waiting for transfers between devices: 23.9 us -> 19 us  [on_device(): others.append(lax.ppermute(own, 'grp', pairs[which][1]))]
  transfers between devices with their start and end apart: 23 -> 23, of which waited for: 15 -> 13; matrix products, arithmetic and copies ran while one was open for 4% -> 4% of each run, Pallas kernels for 16% -> 14%
where the time goes in v1:
time: 332 us; the launch traced here: 330 us
  waiting for transfers between devices  160 us (48%)
  starting transfers between devices  58.2 us (18%)
  Pallas kernels  51 us (15%)
  local copies, waits for them, and re-layouts  29.8 us (9%)
  blocking collectives  17.5 us (5%)
  matrix products  13.6 us (4%)
    ppermute x6, waiting for transfers between devices, on_device(): far_w[which].append(lax.ppermute(w[which], 'grp', pairs[which][0]))  63.7 us
    pallas_call x2, Pallas kernels, experts(): pl.pallas_call(functools.partial(experts_body, sets), out_shape=out_shape...  28.6 us
    all_to_all x3, starting transfers between devices, home(): return lax.all_to_all(rows, 'ctx', 0, 0, tiled=True)  26.2 us
    ppermute x2, waiting for transfers between devices, on_device(): came.append(lax.ppermute(results[which], 'grp', pairs[which][1]))  24.2 us
    ppermute x4, waiting for transfers between devices, on_device(): others.append(lax.ppermute(own, 'grp', pairs[which][1]))  19 us
    unnamed x48, local copies, waits for them, and re-layouts  18.9 us
    all_to_all x2, waiting for transfers between devices, on_device(): lax.all_to_all(buffer.reshape(n_ctx, 2 * half, D), 'ctx', 0, 0, tiled=True)  18.5 us
    all_to_all x1, blocking collectives, on_device(): got = lax.all_to_all(payload, 'ctx', 0, 0, tiled=True)  17.5 us
  transfers between devices with their start and end apart: 23, of which 13 were waited for; matrix products, arithmetic and copies ran while one was open for 4% of the time, Pallas kernels for 14%

profile of v1, /device:TPU:1, one launch (start us, length us, event | category | flops | bytes accessed | tf_op | source)
XLA Modules:
  0.0 330.4 jit_solution(4449520598073957631)
XLA Ops:
  4.8 17.5 %all_to_all.40.got_ref = bf16[32,24,128]{2,1,0:T(8,128)(2,1)S(1)} all-to-all(bf16[32,24,128]{2,1,0:T(8,128)(2,1)S(1)} %local_states.1), channel_id=1, replica_groups=mesh['ctx'=32,'grp'=4] {'ctx'}, dimensions={0} | all-to-all | bytes 393216 | tf_op jit(solution)/shard_map/all_to_all | solution.py:456
  23.3 3.8 %all-to-all-start.1 = ((bf16[32,24,128]{2,1,0:T(8,128)(2,1)}), bf16[32,24,128]{2,1,0:T(8,128)(2,1)S(1)}, u32[]{:S(2)}, u32[]{:S(2)}) async-start(bf16[32,24,128]{2,1,0:T(8,128)(2,1)} %prior_states.1), calls=%async_computation.1 | async-start | bytes 393216 | tf_op jit(solution)/shard_map/all_to_all | solution.py:461
  27.1 5.6 %inner_attention.1 = (f32[512,512]{1,0:T(8,128)}, f32[512,128]{1,0:T(8,128)}) custom-call(bf16[512,512]{1,0:T(8,128)(2,1)} %q_ref.3, bf16[512,512]{1,0:T(8,128)(2,1)} %k_ref.3, bf16[512,512]{1,0:T(8,128)(2,1)} %v_ref.3, f32[4,512]{1,0:T(4,128)} %decay_ref.5), custom_call_target="tpu_custom_call" | custom-call | flops 536870912 | bytes 2097152 | tf_op jit(solution)/shard_map/inner_attention/pallas_call | solution.py:148
  32.8 2.8 all-to-all-done.1.prior_ref
  36.2 3.9 %outer_attention.1 = bf16[4,128,512]{2,1,0:T(8,128)(2,1)} custom-call(bf16[512,512]{1,0:T(8,128)(2,1)} %q_ref.3, f32[4,512]{1,0:T(4,128)} %decay_ref.5, bf16[32,24,128]{2,1,0:T(8,128)(2,1)} %copy-done.21, f32[512,512]{1,0:T(8,128)} %get-tuple-element.15.num_ref, f32[512,128]{1,0:T(8,128)} %get-tuple-element.16.den_ref), custom_call_target="tpu_custom_call" | custom-call | tf_op jit(solution)/shard_map/outer_attention/pallas_call | solution.py:186
  40.1 4.2 %all-to-all-start.2 = ((bf16[4,128,512]{2,1,0:T(8,128)(2,1)}), bf16[4,128,512]{2,1,0:T(8,128)(2,1)S(1)}, u32[]{:S(2)}, u32[]{:S(2)}) async-start(bf16[4,128,512]{2,1,0:T(8,128)(2,1)} %outer_attention.1), calls=%async_computation.2 | async-start | bytes 1048576 | tf_op jit(solution)/shard_map/all_to_all | solution.py:464
  44.6 8.7 %all-to-all-done.2 = bf16[4,128,512]{2,1,0:T(8,128)(2,1)S(1)} async-done(((bf16[4,128,512]{2,1,0:T(8,128)(2,1)}), bf16[4,128,512]{2,1,0:T(8,128)(2,1)S(1)}, u32[]{:S(2)}, u32[]{:S(2)}) %all-to-all-start.2) | async-done | bytes 524320 | tf_op jit(solution)/shard_map/all_to_all | solution.py:464
  53.3 4.8 %fusion.2 = (f32[128]{0:T(128)S(1)}, bf16[128,2048]{1,0:T(8,128)(2,1)S(1)}) fusion(bf16[4,128,512]{2,1,0:T(8,128)(2,1)S(1)} %all-to-all-done.2, bf16[4,512,2048]{2,1,0:T(8,128)(2,1)} %bitcast.53, bf16[128,2048]{1,0:T(8,128)(2,1)S(1)} %copy-done.22), kind=kOutput, calls=%fused_computation.14 | convolution fusion | flops 1075314560 | bytes 9961984 | tf_op jit(solution)/shard_map/gtc,gcd->td/dot_general | solution.py:465
  58.2 2.2 convolution_convert_fusion.1
  60.3 6.1 %all-to-all-start.3 = ((bf16[32,16,2048]{2,1,0:T(8,128)(2,1)}), bf16[32,16,2048]{2,1,0:T(8,128)(2,1)}, u32[]{:S(2)}, u32[]{:S(2)}) async-start(bf16[32,16,2048]{2,1,0:T(8,128)(2,1)} %bitcast.56), calls=%async_computation.3 | async-start | bytes 4194304 | tf_op jit(solution)/shard_map/all_to_all | solution.py:479
  74.2 2.2 convolution_convert_fusion
  76.4 18.5 %all-to-all-done.3.refs_0_ = bf16[32,16,2048]{2,1,0:T(8,128)(2,1)} async-done(((bf16[32,16,2048]{2,1,0:T(8,128)(2,1)}), bf16[32,16,2048]{2,1,0:T(8,128)(2,1)}, u32[]{:S(2)}, u32[]{:S(2)}) %all-to-all-start.3) | async-done | bytes 2097184 | tf_op jit(solution)/shard_map/all_to_all | solution.py:479
  94.9 5.2 %all-to-all-start.5 = ((bf16[32,16,2048]{2,1,0:T(8,128)(2,1)}), bf16[32,16,2048]{2,1,0:T(8,128)(2,1)}, u32[]{:S(2)}, u32[]{:S(2)}) async-start(bf16[32,16,2048]{2,1,0:T(8,128)(2,1)} %bitcast.55), calls=%async_computation.5 | async-start | bytes 4194304 | tf_op jit(solution)/shard_map/all_to_all | solution.py:479
  103.5 28.8 %collective-permute-done.1.refs_5_.refs_7_ = bf16[352,2048]{1,0:T(8,128)(2,1)S(1)} collective-permute-done((bf16[352,2048]{1,0:T(8,128)(2,1)}, bf16[352,2048]{1,0:T(8,128)(2,1)S(1)}, u32[]{:S(2)}, u32[]{:S(2)}) %collective-permute-start.1) | collective-permute-done | bytes 1441824 | tf_op jit(solution)/shard_map/ppermute | solution.py:452
  132.2 4.0 %collective-permute-done.4.refs_8_.refs_10_ = bf16[352,2048]{1,0:T(8,128)(2,1)} collective-permute-done((bf16[352,2048]{1,0:T(8,128)(2,1)}, bf16[352,2048]{1,0:T(8,128)(2,1)}, u32[]{:S(2)}, u32[]{:S(2)}) %collective-permute-start.4) | collective-permute-done | bytes 1441824 | tf_op jit(solution)/shard_map/ppermute | solution.py:452
  136.2 26.9 %collective-permute-done.2.refs_6_.refs_8_ = bf16[352,2048]{1,0:T(8,128)(2,1)S(1)} collective-permute-done((bf16[352,2048]{1,0:T(8,128)(2,1)S(1)}, bf16[352,2048]{1,0:T(8,128)(2,1)S(1)}, u32[]{:S(2)}, u32[]{:S(2)}) %collective-permute-start.2) | collective-permute-done | bytes 1441824 | tf_op jit(solution)/shard_map/ppermute | solution.py:452
  163.1 4.0 %collective-permute-done.5.refs_9_.refs_11_ = bf16[352,2048]{1,0:T(8,128)(2,1)} collective-permute-done((bf16[352,2048]{1,0:T(8,128)(2,1)S(1)}, bf16[352,2048]{1,0:T(8,128)(2,1)}, u32[]{:S(2)}, u32[]{:S(2)}) %collective-permute-start.5) | collective-permute-done | bytes 1441824 | tf_op jit(solution)/shard_map/ppermute | solution.py:452
  167.1 13.5 %experts.2 = bf16[32,16,2048]{2,1,0:T(8,128)(2,1)} custom-call(bf16[32,16,2048]{2,1,0:T(8,128)(2,1)} %all-to-all-done.3.refs_0_, bf16[2,352,2048]{2,1,0:T(8,128)(2,1)} %bitcast.47, bf16[2,352,2048]{2,1,0:T(8,128)(2,1)} %bitcast.50, bf16[2,352,2048]{2,1,0:T(8,128)(2,1)} %refs_5_.1, bf16[352,2048]{1,0:T(8,128)(2,1)} %copy-done.4, bf16[352,2048]{1,0:T(8,128)(2,1)} %copy-done.6, ...), custom_call_target="tpu_custom_call" | custom-call | flops 4429185024 | bytes 21495808 | tf_op jit(solution)/shard_map/experts/pallas_call | solution.py:317
  180.6 8.8 %all-to-all-start.4 = ((bf16[32,16,2048]{2,1,0:T(8,128)(2,1)}), bf16[32,16,2048]{2,1,0:T(8,128)(2,1)S(1)}, u32[]{:S(2)}, u32[]{:S(2)}) async-start(bf16[32,16,2048]{2,1,0:T(8,128)(2,1)} %experts.2), calls=%async_computation.4 | async-start | bytes 4194304 | tf_op jit(solution)/shard_map/all_to_all | solution.py:488
  192.3 3.3 %fusion.18 = (bf16[32,8,2048]{2,1,0:T(8,128)(2,1)}, bf16[32,8,2048]{2,1,0:T(8,128)(2,1)}) fusion(bf16[32,16,2048]{2,1,0:T(8,128)(2,1)} %all-to-all-done.5.refs_0_), kind=kLoop, calls=%fused_computation.28 | loop fusion | bytes 4194304 | tf_op jit(solution)/shard_map/slice | solution.py:484
  198.1 19.0 %collective-permute-done.6.refs_1_ = bf16[32,8,2048]{2,1,0:T(8,128)(2,1)S(1)} collective-permute-done((bf16[32,8,2048]{2,1,0:T(8,128)(2,1)S(1)}, bf16[32,8,2048]{2,1,0:T(8,128)(2,1)S(1)}, u32[]{:S(2)}, u32[]{:S(2)}) %collective-permute-start.6) | collective-permute-done | bytes 1048608 | tf_op jit(solution)/shard_map/ppermute | solution.py:485
  217.1 15.1 %experts.3 = (bf16[32,16,2048]{2,1,0:T(8,128)(2,1)S(1)}, bf16[32,16,2048]{2,1,0:T(8,128)(2,1)}, bf16[2,3,704,2048]{3,2,1,0:T(8,128)(2,1)S(1)}) custom-call(bf16[32,16,2048]{2,1,0:T(8,128)(2,1)} %all-to-all-done.5.refs_0_, bf16[32,8,2048]{2,1,0:T(8,128)(2,1)S(1)} %collective-permute-done.6.refs_1_, bf16[32,8,2048]{2,1,0:T(8,128)(2,1)S(1)} %collective-permute-done.7.refs_2_, ...), custom_call_target="tpu_custom_call" | custom-call | flops 8858370048 | bytes 25690112 | tf_op jit(solution)/shard_map/experts/pallas_call | solution.py:317
  232.2 6.0 %copy-done = bf16[2,3,704,2048]{3,2,1,0:T(8,128)(2,1)} copy-done((bf16[2,3,704,2048]{3,2,1,0:T(8,128)(2,1)}, bf16[2,3,704,2048]{3,2,1,0:T(8,128)(2,1)S(1)}, u32[]{:S(2)}) %copy-start) | copy-done | bytes 17301528
  240.8 8.9 %all-to-all-start.6 = ((bf16[32,16,2048]{2,1,0:T(8,128)(2,1)}), bf16[32,16,2048]{2,1,0:T(8,128)(2,1)S(1)}, u32[]{:S(2)}, u32[]{:S(2)}) async-start(bf16[32,16,2048]{2,1,0:T(8,128)(2,1)} %get-tuple-element.19), calls=%async_computation.6 | async-start | bytes 4194304 | tf_op jit(solution)/shard_map/all_to_all | solution.py:488
  249.8 5.9 %copy-done.1 = bf16[2,3,704,2048]{3,2,1,0:T(8,128)(2,1)S(1)} copy-done((bf16[2,3,704,2048]{3,2,1,0:T(8,128)(2,1)S(1)}, bf16[2,3,704,2048]{3,2,1,0:T(8,128)(2,1)}, u32[]{:S(2)}) %copy-start.1) | copy-done | bytes 17301528
  255.7 6.9 %last_experts.1 = (bf16[256,2048]{1,0:T(8,128)(2,1)S(1)}, bf16[256,2048]{1,0:T(8,128)(2,1)S(1)}) custom-call(bf16[32,8,2048]{2,1,0:T(8,128)(2,1)S(1)} %collective-permute-done.12.xa, bf16[32,8,2048]{2,1,0:T(8,128)(2,1)} %collective-permute-done.13.xb, bf16[2,3,704,2048]{3,2,1,0:T(8,128)(2,1)S(1)} %copy-done.1), custom_call_target="tpu_custom_call" | custom-call | flops 4429185024 | bytes 4194304 | tf_op jit(solution)/shard_map/last_experts/pallas_call | solution.py:352
  264.4 24.0 %collective-permute-done.14.came_a = bf16[256,2048]{1,0:T(8,128)(2,1)S(1)} collective-permute-done((bf16[256,2048]{1,0:T(8,128)(2,1)S(1)}, bf16[256,2048]{1,0:T(8,128)(2,1)S(1)}, u32[]{:S(2)}, u32[]{:S(2)}) %collective-permute-start.14) | collective-permute-done | bytes 1048608 | tf_op jit(solution)/shard_map/ppermute | solution.py:515
  290.7 8.4 %all-to-all-start.7 = ((bf16[32,16,2048]{2,1,0:T(8,128)(2,1)}), bf16[32,16,2048]{2,1,0:T(8,128)(2,1)}, u32[]{:S(2)}, u32[]{:S(2)}) async-start(bf16[32,16,2048]{2,1,0:T(8,128)(2,1)} %merge.1), calls=%async_computation.7 | async-start | bytes 4194304 | tf_op jit(solution)/shard_map/all_to_all | solution.py:488
  300.4 3.5 %collective-permute-done.8.mix_a = bf16[256,128]{1,0:T(8,128)(2,1)S(1)} collective-permute-done((bf16[256,128]{1,0:T(8,128)(2,1)S(1)}, bf16[256,128]{1,0:T(8,128)(2,1)S(1)}, u32[]{:S(2)}, u32[]{:S(2)}) %collective-permute-start.8) | collective-permute-done | bytes 65568 | tf_op jit(solution)/shard_map/ppermute | solution.py:458
  308.3 10.5 %collective-permute-done.10 = bf16[128,2048]{1,0:T(8,128)(2,1)S(1)} collective-permute-done((bf16[128,2048]{1,0:T(8,128)(2,1)S(1)}, bf16[128,2048]{1,0:T(8,128)(2,1)S(1)}, u32[]{:S(2)}, u32[]{:S(2)}) %collective-permute-start.10) | collective-permute-done | bytes 524320 | tf_op jit(solution)/shard_map/ppermute | solution.py:509
  318.8 8.7 %all-to-all-done.7 = bf16[32,16,2048]{2,1,0:T(8,128)(2,1)} async-done(((bf16[32,16,2048]{2,1,0:T(8,128)(2,1)}), bf16[32,16,2048]{2,1,0:T(8,128)(2,1)}, u32[]{:S(2)}, u32[]{:S(2)}) %all-to-all-start.7) | async-done | bytes 2097184 | tf_op jit(solution)/shard_map/all_to_all | solution.py:488
  327.5 2.9 add_convert_fusion
  (84 shorter events, 35.1 us)
Async XLA Ops:
  23.3 12.2 %all-to-all-start.1 = ((bf16[32,24,128]{2,1,0:T(8,128)(2,1)}), bf16[32,24,128]{2,1,0:T(8,128)(2,1)S(1)}, u32[]{:S(2)}, u32[]{:S(2)}) async-start(bf16[32,24,128]{2,1,0:T(8,128)(2,1)} %prior_states.1), calls=%async_computation.1 | async-start | bytes 393216 | tf_op jit(solution)/shard_map/all_to_all | solution.py:461
  32.8 11.5 %copy-start.13 = (s32[128,6]{0,1:T(8,128)S(1)}, s32[128,6]{0,1:T(8,128)}, u32[]{:S(2)}) copy-start(s32[128,6]{0,1:T(8,128)} %param.19) | copy-start | bytes 9220
  32.8 11.5 %copy-start.14 = (f32[128,6]{0,1:T(8,128)S(1)}, f32[128,6]{0,1:T(8,128)}, u32[]{:S(2)}) copy-start(f32[128,6]{0,1:T(8,128)} %param.20) | copy-start | bytes 9220
  32.8 20.5 %copy-start.22 = (bf16[128,2048]{1,0:T(8,128)(2,1)S(1)}, bf16[128,2048]{1,0:T(8,128)(2,1)}, u32[]{:S(2)}) copy-start(bf16[128,2048]{1,0:T(8,128)(2,1)} %param.16) | copy-start | bytes 1572868
  40.1 13.2 %all-to-all-start.2 = ((bf16[4,128,512]{2,1,0:T(8,128)(2,1)}), bf16[4,128,512]{2,1,0:T(8,128)(2,1)S(1)}, u32[]{:S(2)}, u32[]{:S(2)}) async-start(bf16[4,128,512]{2,1,0:T(8,128)(2,1)} %outer_attention.1), calls=%async_computation.2 | async-start | bytes 1048576 | tf_op jit(solution)/shard_map/all_to_all | solution.py:464
  60.3 34.5 %all-to-all-start.3 = ((bf16[32,16,2048]{2,1,0:T(8,128)(2,1)}), bf16[32,16,2048]{2,1,0:T(8,128)(2,1)}, u32[]{:S(2)}, u32[]{:S(2)}) async-start(bf16[32,16,2048]{2,1,0:T(8,128)(2,1)} %bitcast.56), calls=%async_computation.3 | async-start | bytes 4194304 | tf_op jit(solution)/shard_map/all_to_all | solution.py:479
  68.2 34.3 %collective-permute-start = (bf16[352,2048]{1,0:T(8,128)(2,1)}, bf16[352,2048]{1,0:T(8,128)(2,1)S(1)}, u32[]{:S(2)}, u32[]{:S(2)}) collective-permute-start(bf16[352,2048]{1,0:T(8,128)(2,1)} %get-tuple-element.33), channel_id=1, source_target_pairs={{0,1},{1,0},{2,3},{3,2},{4,5},{5,4},{6,7},{7,6},{8,9},{9,8},{10,11... | collective-permute-start | bytes 4325384 | tf_op jit(solution)/shard_map/ppermute | solution.py:452
  71.2 61.0 %collective-permute-start.1 = (bf16[352,2048]{1,0:T(8,128)(2,1)}, bf16[352,2048]{1,0:T(8,128)(2,1)S(1)}, u32[]{:S(2)}, u32[]{:S(2)}) collective-permute-start(bf16[352,2048]{1,0:T(8,128)(2,1)} %get-tuple-element.31), channel_id=1, source_target_pairs={{0,1},{1,0},{2,3},{3,2},{4,5},{5,4},{6,7},{7,6},{8,9},{9,8},{10,11... | collective-permute-start | bytes 4325384 | tf_op jit(solution)/shard_map/ppermute | solution.py:452
  71.6 60.7 %collective-permute-start.3 = (bf16[352,2048]{1,0:T(8,128)(2,1)}, bf16[352,2048]{1,0:T(8,128)(2,1)}, u32[]{:S(2)}, u32[]{:S(2)}) collective-permute-start(bf16[352,2048]{1,0:T(8,128)(2,1)} %get-tuple-element.32), channel_id=1, source_target_pairs={{0,3},{3,0},{1,2},{2,1},{4,7},{7,4},{5,6},{6,5},{8,11},{11,8},{9,1... | collective-permute-start | bytes 4325384 | tf_op jit(solution)/shard_map/ppermute | solution.py:452
  72.4 63.8 %collective-permute-start.4 = (bf16[352,2048]{1,0:T(8,128)(2,1)}, bf16[352,2048]{1,0:T(8,128)(2,1)}, u32[]{:S(2)}, u32[]{:S(2)}) collective-permute-start(bf16[352,2048]{1,0:T(8,128)(2,1)} %get-tuple-element.30), channel_id=1, source_target_pairs={{0,3},{3,0},{1,2},{2,1},{4,7},{7,4},{5,6},{6,5},{8,11},{11,8},{9,1... | collective-permute-start | bytes 4325384 | tf_op jit(solution)/shard_map/ppermute | solution.py:452
  94.9 85.8 %all-to-all-start.5 = ((bf16[32,16,2048]{2,1,0:T(8,128)(2,1)}), bf16[32,16,2048]{2,1,0:T(8,128)(2,1)}, u32[]{:S(2)}, u32[]{:S(2)}) async-start(bf16[32,16,2048]{2,1,0:T(8,128)(2,1)} %bitcast.55), calls=%async_computation.5 | async-start | bytes 4194304 | tf_op jit(solution)/shard_map/all_to_all | solution.py:479
  102.2 60.9 %collective-permute-start.2 = (bf16[352,2048]{1,0:T(8,128)(2,1)S(1)}, bf16[352,2048]{1,0:T(8,128)(2,1)S(1)}, u32[]{:S(2)}, u32[]{:S(2)}) collective-permute-start(bf16[352,2048]{1,0:T(8,128)(2,1)S(1)} %get-tuple-element.29), channel_id=1, source_target_pairs={{0,1},{1,0},{2,3},{3,2},{4,5},{5,4},{6,7},{7,6},{8,9},{9,8},{10,11... | collective-permute-start | bytes 4325384 | tf_op jit(solution)/shard_map/ppermute | solution.py:452
  102.6 64.6 %copy-start.4 = (bf16[352,2048]{1,0:T(8,128)(2,1)}, bf16[352,2048]{1,0:T(8,128)(2,1)S(1)}, u32[]{:S(2)}) copy-start(bf16[352,2048]{1,0:T(8,128)(2,1)S(1)} %collective-permute-done.refs_4_.refs_6_) | copy-start | bytes 4325380
  102.6 64.6 %collective-permute-start.5 = (bf16[352,2048]{1,0:T(8,128)(2,1)S(1)}, bf16[352,2048]{1,0:T(8,128)(2,1)}, u32[]{:S(2)}, u32[]{:S(2)}) collective-permute-start(bf16[352,2048]{1,0:T(8,128)(2,1)S(1)} %get-tuple-element.28), channel_id=1, source_target_pairs={{0,3},{3,0},{1,2},{2,1},{4,7},{7,4},{5,6},{6,5},{8,11},{11,8},{9,1... | collective-permute-start | bytes 4325384 | tf_op jit(solution)/shard_map/ppermute | solution.py:452
  132.2 34.9 %copy-start.6 = (bf16[352,2048]{1,0:T(8,128)(2,1)}, bf16[352,2048]{1,0:T(8,128)(2,1)S(1)}, u32[]{:S(2)}) copy-start(bf16[352,2048]{1,0:T(8,128)(2,1)S(1)} %collective-permute-done.1.refs_5_.refs_7_) | copy-start | bytes 4325380
  180.6 58.9 %all-to-all-start.4 = ((bf16[32,16,2048]{2,1,0:T(8,128)(2,1)}), bf16[32,16,2048]{2,1,0:T(8,128)(2,1)S(1)}, u32[]{:S(2)}, u32[]{:S(2)}) async-start(bf16[32,16,2048]{2,1,0:T(8,128)(2,1)} %experts.2), calls=%async_computation.4 | async-start | bytes 4194304 | tf_op jit(solution)/shard_map/all_to_all | solution.py:488
  189.5 27.6 %copy-start.9 = (bf16[352,2048]{1,0:T(8,128)(2,1)S(1)}, bf16[352,2048]{1,0:T(8,128)(2,1)}, u32[]{:S(2)}) copy-start(bf16[352,2048]{1,0:T(8,128)(2,1)} %copy-done.8) | copy-start | bytes 4325380
  191.3 25.8 %collective-permute-start.6 = (bf16[32,8,2048]{2,1,0:T(8,128)(2,1)S(1)}, bf16[32,8,2048]{2,1,0:T(8,128)(2,1)S(1)}, u32[]{:S(2)}, u32[]{:S(2)}) collective-permute-start(bf16[32,8,2048]{2,1,0:T(8,128)(2,1)S(1)} %get-tuple-element.37), channel_id=1, source_target_pairs={{0,3},{3,0},{1,2},{2,1},{4,7},{7,4},{5,6},{6,5},{8,11},{11,8},{9,1... | collective-permute-start | bytes 3145736 | tf_op jit(solution)/shard_map/ppermute | solution.py:485
  192.3 24.8 %copy-start.5 = (bf16[352,2048]{1,0:T(8,128)(2,1)S(1)}, bf16[352,2048]{1,0:T(8,128)(2,1)}, u32[]{:S(2)}) copy-start(bf16[352,2048]{1,0:T(8,128)(2,1)} %copy-done.4) | copy-start | bytes 4325380
  192.3 24.8 %copy-start.7 = (bf16[352,2048]{1,0:T(8,128)(2,1)S(1)}, bf16[352,2048]{1,0:T(8,128)(2,1)}, u32[]{:S(2)}) copy-start(bf16[352,2048]{1,0:T(8,128)(2,1)} %copy-done.6) | copy-start | bytes 4325380
  192.3 24.8 %collective-permute-start.7 = (bf16[32,8,2048]{2,1,0:T(8,128)(2,1)S(1)}, bf16[32,8,2048]{2,1,0:T(8,128)(2,1)S(1)}, u32[]{:S(2)}, u32[]{:S(2)}) collective-permute-start(bf16[32,8,2048]{2,1,0:T(8,128)(2,1)S(1)} %get-tuple-element.36), channel_id=1, source_target_pairs={{0,1},{1,0},{2,3},{3,2},{4,5},{5,4},{6,7},{7,6},{8,9},{9,8},{10,11... | collective-permute-start | bytes 3145736 | tf_op jit(solution)/shard_map/ppermute | solution.py:485
  195.6 54.1 %collective-permute-start.12 = (bf16[32,8,2048]{2,1,0:T(8,128)(2,1)}, bf16[32,8,2048]{2,1,0:T(8,128)(2,1)S(1)}, u32[]{:S(2)}, u32[]{:S(2)}) collective-permute-start(bf16[32,8,2048]{2,1,0:T(8,128)(2,1)} %get-tuple-element.35), channel_id=1, source_target_pairs={{0,3},{3,0},{1,2},{2,1},{4,7},{7,4},{5,6},{6,5},{8,11},{11,8},{9,1... | collective-permute-start | bytes 3145736 | tf_op jit(solution)/shard_map/ppermute | solution.py:485
  197.4 52.4 %collective-permute-start.13 = (bf16[32,8,2048]{2,1,0:T(8,128)(2,1)}, bf16[32,8,2048]{2,1,0:T(8,128)(2,1)}, u32[]{:S(2)}, u32[]{:S(2)}) collective-permute-start(bf16[32,8,2048]{2,1,0:T(8,128)(2,1)} %get-tuple-element.34), channel_id=1, source_target_pairs={{0,1},{1,0},{2,3},{3,2},{4,5},{5,4},{6,7},{7,6},{8,9},{9,8},{10,11... | collective-permute-start | bytes 3145736 | tf_op jit(solution)/shard_map/ppermute | solution.py:485
  240.8 49.9 %all-to-all-start.6 = ((bf16[32,16,2048]{2,1,0:T(8,128)(2,1)}), bf16[32,16,2048]{2,1,0:T(8,128)(2,1)S(1)}, u32[]{:S(2)}, u32[]{:S(2)}) async-start(bf16[32,16,2048]{2,1,0:T(8,128)(2,1)} %get-tuple-element.19), calls=%async_computation.6 | async-start | bytes 4194304 | tf_op jit(solution)/shard_map/all_to_all | solution.py:488
  255.7 32.9 %copy-start.3 = (bf16[32,16,2048]{2,1,0:T(8,128)(2,1)S(1)}, bf16[32,16,2048]{2,1,0:T(8,128)(2,1)}, u32[]{:S(2)}) copy-start(bf16[32,16,2048]{2,1,0:T(8,128)(2,1)} %copy-done.2) | copy-start | bytes 6291460
  262.6 25.8 %collective-permute-start.14 = (bf16[256,2048]{1,0:T(8,128)(2,1)S(1)}, bf16[256,2048]{1,0:T(8,128)(2,1)S(1)}, u32[]{:S(2)}, u32[]{:S(2)}) collective-permute-start(bf16[256,2048]{1,0:T(8,128)(2,1)S(1)} %get-tuple-element.26), channel_id=1, source_target_pairs={{0,3},{3,0},{1,2},{2,1},{4,7},{7,4},{5,6},{6,5},{8,11},{11,8},{9,1... | collective-permute-start | bytes 3145736 | tf_op jit(solution)/shard_map/ppermute | solution.py:515
  264.4 24.2 %collective-permute-start.15 = (bf16[256,2048]{1,0:T(8,128)(2,1)S(1)}, bf16[256,2048]{1,0:T(8,128)(2,1)S(1)}, u32[]{:S(2)}, u32[]{:S(2)}) collective-permute-start(bf16[256,2048]{1,0:T(8,128)(2,1)S(1)} %get-tuple-element.27), channel_id=1, source_target_pairs={{0,1},{1,0},{2,3},{3,2},{4,5},{5,4},{6,7},{7,6},{8,9},{9,8},{10,11... | collective-permute-start | bytes 3145736 | tf_op jit(solution)/shard_map/ppermute | solution.py:515
  290.7 36.8 %all-to-all-start.7 = ((bf16[32,16,2048]{2,1,0:T(8,128)(2,1)}), bf16[32,16,2048]{2,1,0:T(8,128)(2,1)}, u32[]{:S(2)}, u32[]{:S(2)}) async-start(bf16[32,16,2048]{2,1,0:T(8,128)(2,1)} %merge.1), calls=%async_computation.7 | async-start | bytes 4194304 | tf_op jit(solution)/shard_map/all_to_all | solution.py:488
  299.1 4.8 %collective-permute-start.8 = (bf16[256,128]{1,0:T(8,128)(2,1)S(1)}, bf16[256,128]{1,0:T(8,128)(2,1)S(1)}, u32[]{:S(2)}, u32[]{:S(2)}) collective-permute-start(bf16[256,128]{1,0:T(8,128)(2,1)S(1)} %get-tuple-element.20), channel_id=1, source_target_pairs={{0,3},{3,0},{1,2},{2,1},{4,7},{7,4},{5,6},{6,5},{8,11},{11,8},{9,1... | collective-permute-start | bytes 196616 | tf_op jit(solution)/shard_map/ppermute | solution.py:458
  300.4 3.5 %collective-permute-start.9 = (bf16[256,128]{1,0:T(8,128)(2,1)S(1)}, bf16[256,128]{1,0:T(8,128)(2,1)S(1)}, u32[]{:S(2)}, u32[]{:S(2)}) collective-permute-start(bf16[256,128]{1,0:T(8,128)(2,1)S(1)} %get-tuple-element.21), channel_id=1, source_target_pairs={{0,1},{1,0},{2,3},{3,2},{4,5},{5,4},{6,7},{7,6},{8,9},{9,8},{10,11... | collective-permute-start | bytes 196616 | tf_op jit(solution)/shard_map/ppermute | solution.py:459
  305.2 13.5 %collective-permute-start.10 = (bf16[128,2048]{1,0:T(8,128)(2,1)S(1)}, bf16[128,2048]{1,0:T(8,128)(2,1)S(1)}, u32[]{:S(2)}, u32[]{:S(2)}) collective-permute-start(bf16[128,2048]{1,0:T(8,128)(2,1)S(1)} %get-tuple-element.22), channel_id=1, source_target_pairs={{0,3},{3,0},{1,2},{2,1},{4,7},{7,4},{5,6},{6,5},{8,11},{11,8},{9,1... | collective-permute-start | bytes 1572872 | tf_op jit(solution)/shard_map/ppermute | solution.py:509
  306.8 12.0 %collective-permute-start.11 = (bf16[128,2048]{1,0:T(8,128)(2,1)S(1)}, bf16[128,2048]{1,0:T(8,128)(2,1)S(1)}, u32[]{:S(2)}, u32[]{:S(2)}) collective-permute-start(bf16[128,2048]{1,0:T(8,128)(2,1)S(1)} %get-tuple-element.23), channel_id=1, source_target_pairs={{0,1},{1,0},{2,3},{3,2},{4,5},{5,4},{6,7},{7,6},{8,9},{9,8},{10,11... | collective-permute-start | bytes 1572872 | tf_op jit(solution)/shard_map/ppermute | solution.py:510
  (15 other events, 50.6 us)

commit v2 on v1

--- a/solution.py
+++ b/solution.py
@@ -16,11 +16,13 @@
 CHUNKS = 2
 EXTRA = 8
 GRANT = 58 << 20
-KEEP_GRANT = 24 << 20
+KEEP_GRANT = 16 << 20
 FAR = [(0, 3), (3, 0), (1, 2), (2, 1)]
 NEAR = [(0, 1), (1, 0), (2, 3), (3, 2)]
 F32 = jnp.float32
 BF16 = jnp.bfloat16
+ANYWHERE = pl.BlockSpec(memory_space=pl.ANY)
+ON_CHIP = pl.BlockSpec(memory_space=pltpu.VMEM)
 
 
 def feature(values):
@@ -42,12 +44,40 @@
     return jnp.concatenate([decay, jnp.zeros((8 - decay.shape[0], decay.shape[1]), F32)], axis=0)
 
 
-def state_body(k_ref, v_ref, decay_ref, out_ref):
+class Parting:
+    def __init__(self, both, parts, held, sems):
+        self.load = pltpu.make_async_copy(both, held, sems.at[0])
+        self.stores = [
+            pltpu.make_async_copy(held.at[e], parts[e], sems.at[1 + e]) for e in range(2)
+        ]
+        self.load.start()
+
+    def turn(self):
+        self.load.wait()
+        for store in self.stores:
+            store.start()
+
+    def finish(self):
+        for store in self.stores:
+            store.wait()
+
+
+def parting_scratch(both):
+    return [pltpu.VMEM(both.shape, BF16), pltpu.SemaphoreType.DMA((3,))]
+
+
+def parts_of(both):
+    return [jax.ShapeDtypeStruct(both.shape[1:], BF16)] * 2
+
+
+def state_body(k_ref, v_ref, decay_ref, w_ref, out_ref, wa_ref, wb_ref, held, sems):
+    parting = Parting(w_ref, (wa_ref, wb_ref), held, sems)
     heads, length = decay_ref.shape
     cum = running_sum(padded_decay(decay_ref))
     total = cum[:, length - 1 :]
     fade = jnp.exp(total - cum).T
     parts = out_ref.shape[0] // heads
+    parting.turn()
     row = lax.broadcasted_iota(jnp.int32, (EXTRA, HD), 0)
     for h in range(heads):
         cols = slice(h * HD, (h + 1) * HD)
@@ -69,15 +99,19 @@
         out_ref[h * parts : (h + 1) * parts, SLOTS:, :] = jnp.broadcast_to(
             extra.astype(BF16)[None], (parts, EXTRA, HD)
         )
-
-
-def local_states(keys, values, decay, blocks):
+    parting.finish()
+
+
+def local_states(keys, values, decay, blocks, both):
     return pl.pallas_call(
         state_body,
-        out_shape=jax.ShapeDtypeStruct((blocks, SLOTS + EXTRA, HD), BF16),
-        compiler_params=pltpu.CompilerParams(vmem_limit_bytes=8 << 20),
+        out_shape=[jax.ShapeDtypeStruct((blocks, SLOTS + EXTRA, HD), BF16), *parts_of(both)],
+        in_specs=[ON_CHIP] * 3 + [ANYWHERE],
+        out_specs=[ON_CHIP, ANYWHERE, ANYWHERE],
+        scratch_shapes=parting_scratch(both),
+        compiler_params=pltpu.CompilerParams(vmem_limit_bytes=GRANT),
         name="local_states",
-    )(keys, values, decay)
+    )(keys, values, decay, both)
 
 
 def prior_body(got_ref, out_ref):
@@ -113,7 +147,8 @@
     )(got)
 
 
-def inner_body(q_ref, k_ref, v_ref, decay_ref, num_ref, den_ref):
+def inner_body(q_ref, k_ref, v_ref, decay_ref, w_ref, num_ref, den_ref, wa_ref, wb_ref, held, sems):
+    parting = Parting(w_ref, (wa_ref, wb_ref), held, sems)
     heads, length = decay_ref.shape
     cum = running_sum(padded_decay(decay_ref))
     cum_col = cum.T
@@ -125,6 +160,8 @@
         col = lax.broadcasted_iota(jnp.int32, (tile, seen), 1)
         at = lax.broadcasted_iota(jnp.int32, (tile, seen), 0) + t * tile
         causal = col <= at
+        if t == 1:
+            parting.turn()
         dens = jnp.zeros((tile, HD), F32)
         for h in range(heads):
             cols = slice(h * HD, (h + 1) * HD)
@@ -141,16 +178,21 @@
                 weights.astype(BF16), v_ref[0:seen, cols], preferred_element_type=F32
             )
         den_ref[rows, :] = dens
-
-
-def inner_attention(queries, keys, values, decay):
+    parting.finish()
+
+
+def inner_attention(queries, keys, values, decay, both):
     length, width = queries.shape
     return pl.pallas_call(
         inner_body,
         out_shape=[
             jax.ShapeDtypeStruct((length, width), F32),
             jax.ShapeDtypeStruct((length, HD), F32),
+            *parts_of(both),
         ],
+        in_specs=[ON_CHIP] * 4 + [ANYWHERE],
+        out_specs=[ON_CHIP, ON_CHIP, ANYWHERE, ANYWHERE],
+        scratch_shapes=parting_scratch(both),
         cost_estimate=pl.CostEstimate(
             flops=4 * length * length * width,
             bytes_accessed=8 * length * width,
@@ -158,7 +200,7 @@
         ),
         compiler_params=pltpu.CompilerParams(vmem_limit_bytes=GRANT),
         name="inner_attention",
-    )(queries, keys, values, decay)
+    )(queries, keys, values, decay, both)
 
 
 def outer_body(q_ref, decay_ref, prior_ref, num_ref, den_ref, out_ref):
@@ -186,12 +228,14 @@
     return pl.pallas_call(
         outer_body,
         out_shape=jax.ShapeDtypeStruct((groups, length // groups, width), BF16),
-        compiler_params=pltpu.CompilerParams(vmem_limit_bytes=GRANT),
+        compiler_params=pltpu.CompilerParams(vmem_limit_bytes=50 << 20),
         name="outer_attention",
     )(queries, decay, prior, num, den)
 
 
-def route_body(ids_ref, gates_ref, dispatch_ref, combine_ref, even_ref, odd_ref):
+def route_body(ids_ref, gates_ref, w_ref, *refs):
+    dispatch_ref, combine_ref, even_ref, odd_ref, wa_ref, wb_ref, held, sems = refs
+    parting = Parting(w_ref, (wa_ref, wb_ref), held, sems)
     rows = ids_ref.shape[1]
     expert = lax.broadcasted_iota(jnp.int32, (E, rows), 0)
     hits = jnp.zeros((E, rows), F32)
@@ -208,6 +252,7 @@
     slot = jnp.where(hits > 0.0, slot, -1.0)
     gates = gates.astype(BF16).astype(F32)
     half = SLOTS // CHUNKS
+    parting.turn()
     for chunk in range(CHUNKS):
         place = lax.broadcasted_iota(jnp.int32, (E, half, rows), 1) + chunk * half
         here = jnp.broadcast_to(slot[:, None, :], (E, half, rows)) == place.astype(F32)
@@ -218,17 +263,21 @@
             by_parity = mix.reshape(E // 2, 2, half, rows)
             for parity, ref in ((0, even_ref), (1, odd_ref)):
                 ref[...] = by_parity[:, parity].reshape(E // 2 * half, rows).astype(BF16)
-
-
-def route(ids, gates):
+    parting.finish()
+
+
+def route(ids, gates, both):
     rows = ids.shape[1]
     shape = jax.ShapeDtypeStruct((CHUNKS, E * SLOTS // CHUNKS, rows), BF16)
     part = jax.ShapeDtypeStruct((E // 2 * SLOTS // CHUNKS, rows), BF16)
     return pl.pallas_call(
         route_body,
-        out_shape=[shape, shape, part, part], compiler_params=pltpu.CompilerParams(vmem_limit_bytes=4 << 20),
+        out_shape=[shape, shape, part, part, *parts_of(both)],
+        in_specs=[ON_CHIP, ON_CHIP, ANYWHERE],
+        out_specs=[ON_CHIP] * 4 + [ANYWHERE] * 2,
+        scratch_shapes=parting_scratch(both), compiler_params=pltpu.CompilerParams(vmem_limit_bytes=GRANT),
         name="route",
-    )(ids, gates)
+    )(ids, gates, both)
 
 
 NT = (((1,), (1,)), ((), ()))
@@ -325,38 +374,20 @@
     )(*xs, *own, *fars[0], *fars[1])
 
 
-def last_body(xa, xb, weights, out_a, out_b, xs, sems):
-    outs = (out_a, out_b)
-    for e, x_ref in enumerate((xa, xb)):
-        pltpu.make_async_copy(x_ref, xs.at[e], sems.at[e]).start()
-
-    def expert(e, carry):
-        def emit(cols, part):
-            for k in range(2):
-
-                @pl.when(e == k)
-                def _():
-                    outs[k][:, cols] = part
-
-        pltpu.make_async_copy(xa, xs.at[e], sems.at[e]).wait()
-        expert_rows(xs[e].reshape(-1, D), weights, e, lambda i: None, emit)
-        return carry
-
-    lax.fori_loop(0, 2, expert, 0)
+def last_body(xa, xb, weights, out_a, out_b):
+    for e, (x_ref, out) in enumerate(((xa, out_a), (xb, out_b))):
+
+        def emit(cols, part, out=out):
+            out[:, cols] = part
+
+        expert_rows(x_ref[...].reshape(-1, D), weights, e, lambda i: None, emit)
 
 
 def last_experts(xa, xb, weights):
     blocks, rows, _ = xa.shape
-    anywhere = pl.BlockSpec(memory_space=pl.ANY)
-    on_chip = pl.BlockSpec(memory_space=pltpu.VMEM)
     return pl.pallas_call(
         last_body,
         out_shape=[jax.ShapeDtypeStruct((blocks * rows, D), BF16)] * 2,
-        in_specs=[anywhere, anywhere, on_chip],
-        scratch_shapes=[
-            pltpu.VMEM((2, blocks, rows, D), BF16),
-            pltpu.SemaphoreType.DMA((2,)),
-        ],
         compiler_params=pltpu.CompilerParams(vmem_limit_bytes=KEEP_GRANT),
         cost_estimate=expert_cost(2 * blocks * rows, weights.shape[2] // 2, 0),
         name="last_experts",
@@ -446,21 +477,29 @@
     up_t = jnp.swapaxes(up_proj, 1, 2)
     pairs = ((NEAR, FAR), (FAR, NEAR))
     own_w = (gate_t, up_t, down_proj)
-    far_w = [[], []]
-    for w in (gate_t, up_t, down_proj):
+
+    def send(parts):
+        far = []
         for which in range(2):
-            far_w[which].append(lax.ppermute(w[which], "grp", pairs[which][0]))
+            far.append(lax.ppermute(parts[which], "grp", pairs[which][0]))
+        return far
 
     n_grp = lax.axis_size("grp")
-    payload = local_states(key_heads, value_heads, log_decay, n_ctx)
+    payload, *gates = local_states(key_heads, value_heads, log_decay, n_ctx, gate_t)
+    far_gate = send(gates)
     got = lax.all_to_all(payload, "ctx", 0, 0, tiled=True)
-    dispatch, combine, even, odd = route(jnp.swapaxes(expert_ids, 0, 1), jnp.swapaxes(gate_weights, 0, 1))
+    dispatch, combine, even, odd, *downs = route(
+        jnp.swapaxes(expert_ids, 0, 1), jnp.swapaxes(gate_weights, 0, 1), down_proj
+    )
     far_even = lax.ppermute(even, "grp", FAR)
     near_odd = lax.ppermute(odd, "grp", NEAR)
     back = prior_states(got)
     prior = lax.all_to_all(back, "ctx", 0, 0, tiled=True)
-    num, den = inner_attention(query_heads, key_heads, value_heads, log_decay)
+    num, den, *ups = inner_attention(
+        query_heads, key_heads, value_heads, log_decay, up_t
+    )
     mixed = outer_attention(query_heads, log_decay, prior, num, den, n_grp)
+    far_w = list(zip(far_gate, send(ups), send(downs)))
     heads_in = lax.all_to_all(mixed, "grp", 0, 0, tiled=True)
     projected = jnp.einsum(
         "gtc,gcd->td", heads_in, out_weight.reshape(n_grp, -1, D), preferred_element_type=F32

time: 332 us -> 364 us (1.096)
  waiting for transfers between devices: 160 us -> 189 us
  Pallas kernels: 51 us -> 58.5 us
  local copies, waits for them, and re-layouts: 29.8 us -> 22.3 us
    ppermute x6, waiting for transfers between devices: 63.7 us -> 91.7 us  [send(): far.append(lax.ppermute(parts[which], 'grp', pairs[which][0]))]
    pallas_call x2, Pallas kernels: 1.63 us -> 10.2 us  [the longest x1 5.28 us: local_states(): pl.pallas_call(state_body, out_shape=[jax.ShapeDtypeStruct((blocks, SLOTS...]
    all_to_all x2, waiting for transfers between devices: 18.5 us -> 24.7 us  [on_device(): lax.all_to_all(buffer.reshape(n_ctx, 2 * half, D), 'ctx', 0, 0, tiled=True)]
    squeeze x3 -> x0, local copies, waits for them, and re-layouts: 5.75 us -> none  [on_device(): far_w[which].append(lax.ppermute(w[which], 'grp', pairs[which][0]))]
    all_to_all x1, waiting for transfers between devices: 8.74 us -> 4.02 us  [on_device(): heads_in = lax.all_to_all(mixed, 'grp', 0, 0, tiled=True)]
    unnamed x48 -> x46, local copies, waits for them, and re-layouts: 18.9 us -> 19 us
  transfers between devices with their start and end apart: 23 -> 23, of which waited for: 13 -> 12; matrix products, arithmetic and copies ran while one was open for 4% -> 2% of each run, Pallas kernels for 14% -> 14%
where the time goes in v2:
time: 364 us; the launch traced here: 362 us
  waiting for transfers between devices  189 us (52%)
  Pallas kernels  58.5 us (16%)
  starting transfers between devices  58.2 us (16%)
  local copies, waits for them, and re-layouts  22.3 us (6%)
  blocking collectives  17.7 us (5%)
  matrix products  15.2 us (4%)
    ppermute x6, waiting for transfers between devices, send(): far.append(lax.ppermute(parts[which], 'grp', pairs[which][0]))  91.7 us
    pallas_call x2, Pallas kernels, experts(): pl.pallas_call(functools.partial(experts_body, sets), out_shape=out_shape...  27.4 us
    all_to_all x3, starting transfers between devices, home(): return lax.all_to_all(rows, 'ctx', 0, 0, tiled=True)  25.9 us
    all_to_all x2, waiting for transfers between devices, on_device(): lax.all_to_all(buffer.reshape(n_ctx, 2 * half, D), 'ctx', 0, 0, tiled=True)  24.7 us
    ppermute x2, waiting for transfers between devices, on_device(): came.append(lax.ppermute(results[which], 'grp', pairs[which][1]))  24.2 us
    ppermute x4, waiting for transfers between devices, on_device(): others.append(lax.ppermute(own, 'grp', pairs[which][1]))  20.6 us
    unnamed x46, local copies, waits for them, and re-layouts  19 us
    all_to_all x1, blocking collectives, on_device(): got = lax.all_to_all(payload, 'ctx', 0, 0, tiled=True)  17.7 us
  transfers between devices with their start and end apart: 23, of which 12 were waited for; matrix products, arithmetic and copies ran while one was open for 2% of the time, Pallas kernels for 14%

profile of v2, /device:TPU:1, one launch (start us, length us, event | category | flops | bytes accessed | tf_op | source)
XLA Modules:
  0.0 362.4 jit_solution(4875890020866928309)
XLA Ops:
  0.6 5.3 %local_states.1 = (bf16[32,24,128]{2,1,0:T(8,128)(2,1)}, bf16[352,2048]{1,0:T(8,128)(2,1)}, bf16[352,2048]{1,0:T(8,128)(2,1)}) custom-call(bf16[512,512]{1,0:T(8,128)(2,1)} %k_ref.3, bf16[512,512]{1,0:T(8,128)(2,1)} %v_ref.3, f32[4,512]{1,0:T(4,128)} %decay_ref.5, bf16[2,352,2048]{2,1,0:T(8,128)(2,1)} %bitcast.33), custom_call_target="tpu_custom_call" | custom-call | tf_op jit(solution)/shard_map/local_states/pallas_call | solution.py:106
  5.9 17.7 %all_to_all.40.got_ref = bf16[32,24,128]{2,1,0:T(8,128)(2,1)S(1)} all-to-all(bf16[32,24,128]{2,1,0:T(8,128)(2,1)} %get-tuple-element.22), channel_id=1, replica_groups=mesh['ctx'=32,'grp'=4] {'ctx'}, dimensions={0} | all-to-all | bytes 393216 | tf_op jit(solution)/shard_map/all_to_all | solution.py:490
  24.6 3.8 %all-to-all-start.1 = ((bf16[32,24,128]{2,1,0:T(8,128)(2,1)}), bf16[32,24,128]{2,1,0:T(8,128)(2,1)S(1)}, u32[]{:S(2)}, u32[]{:S(2)}) async-start(bf16[32,24,128]{2,1,0:T(8,128)(2,1)} %prior_states.1), calls=%async_computation.1 | async-start | bytes 393216 | tf_op jit(solution)/shard_map/all_to_all | solution.py:497
  28.5 6.3 %inner_attention.1 = (f32[512,512]{1,0:T(8,128)}, f32[512,128]{1,0:T(8,128)}, bf16[352,2048]{1,0:T(8,128)(2,1)}, bf16[352,2048]{1,0:T(8,128)(2,1)}) custom-call(bf16[512,512]{1,0:T(8,128)(2,1)} %q_ref.3, bf16[512,512]{1,0:T(8,128)(2,1)} %k_ref.3, bf16[512,512]{1,0:T(8,128)(2,1)} %v_ref.3, f32[4,512]{1,0:T(4,128)} %decay_ref.5, bf16[2,352,2048]{2,1,0:T(8,128)(2,1)} %bitcast.36), custom_call_target="tpu_custom_call" | custom-call | flops 536870912 | bytes 2097152 | tf_op jit(solution)/shard_map/inner_attention/pallas_call | solution.py:186
  34.8 2.1 all-to-all-done.1.prior_ref
  39.0 2.4 outer_attention.1
  41.4 4.3 %all-to-all-start.2 = ((bf16[4,128,512]{2,1,0:T(8,128)(2,1)}), bf16[4,128,512]{2,1,0:T(8,128)(2,1)S(1)}, u32[]{:S(2)}, u32[]{:S(2)}) async-start(bf16[4,128,512]{2,1,0:T(8,128)(2,1)} %outer_attention.1), calls=%async_computation.2 | async-start | bytes 1048576 | tf_op jit(solution)/shard_map/all_to_all | solution.py:503
  45.8 5.0 %route.1 = (bf16[2,512,128]{2,1,0:T(8,128)(2,1)}, bf16[2,512,128]{2,1,0:T(8,128)(2,1)}, bf16[256,128]{1,0:T(8,128)(2,1)}, bf16[256,128]{1,0:T(8,128)(2,1)}, bf16...) custom-call(s32[6,128]{1,0:T(8,128)} %bitcast.42, f32[6,128]{1,0:T(8,128)} %bitcast.43, bf16[2,352,2048]{2,1,0:T(8,128)(2,1)} %refs_5_.1), custom_call_target="tpu_custom_call" | custom-call | tf_op jit(solution)/shard_map/route/pallas_call | solution.py:273
  50.7 4.0 %all-to-all-done.2 = bf16[4,128,512]{2,1,0:T(8,128)(2,1)S(1)} async-done(((bf16[4,128,512]{2,1,0:T(8,128)(2,1)}), bf16[4,128,512]{2,1,0:T(8,128)(2,1)S(1)}, u32[]{:S(2)}, u32[]{:S(2)}) %all-to-all-start.2) | async-done | bytes 524320 | tf_op jit(solution)/shard_map/all_to_all | solution.py:503
  54.8 4.8 %fusion.2 = (f32[128]{0:T(128)S(1)}, bf16[128,2048]{1,0:T(8,128)(2,1)S(1)}) fusion(bf16[4,128,512]{2,1,0:T(8,128)(2,1)S(1)} %all-to-all-done.2, bf16[4,512,2048]{2,1,0:T(8,128)(2,1)} %bitcast.39, bf16[128,2048]{1,0:T(8,128)(2,1)S(1)} %copy-done.17), kind=kOutput, calls=%fused_computation.8 | convolution fusion | flops 1075314560 | bytes 9961984 | tf_op jit(solution)/shard_map/gtc,gcd->td/dot_general | solution.py:504
  60.4 2.2 convolution_convert_fusion.1
  62.6 6.5 %all-to-all-start.3 = ((bf16[32,16,2048]{2,1,0:T(8,128)(2,1)}), bf16[32,16,2048]{2,1,0:T(8,128)(2,1)S(1)}, u32[]{:S(2)}, u32[]{:S(2)}) async-start(bf16[32,16,2048]{2,1,0:T(8,128)(2,1)} %bitcast.41), calls=%async_computation.3 | async-start | bytes 4194304 | tf_op jit(solution)/shard_map/all_to_all | solution.py:518
  69.4 3.3 convolution_convert_fusion
  72.7 24.7 %all-to-all-done.3.refs_0_ = bf16[32,16,2048]{2,1,0:T(8,128)(2,1)S(1)} async-done(((bf16[32,16,2048]{2,1,0:T(8,128)(2,1)}), bf16[32,16,2048]{2,1,0:T(8,128)(2,1)S(1)}, u32[]{:S(2)}, u32[]{:S(2)}) %all-to-all-start.3) | async-done | bytes 2097184 | tf_op jit(solution)/shard_map/all_to_all | solution.py:518
  98.8 4.5 %all-to-all-start.5 = ((bf16[32,16,2048]{2,1,0:T(8,128)(2,1)}), bf16[32,16,2048]{2,1,0:T(8,128)(2,1)S(1)}, u32[]{:S(2)}, u32[]{:S(2)}) async-start(bf16[32,16,2048]{2,1,0:T(8,128)(2,1)} %bitcast.40), calls=%async_computation.5 | async-start | bytes 4194304 | tf_op jit(solution)/shard_map/all_to_all | solution.py:518
  107.8 29.8 %collective-permute-done.4.refs_8_.refs_10_ = bf16[352,2048]{1,0:T(8,128)(2,1)S(1)} collective-permute-done((bf16[352,2048]{1,0:T(8,128)(2,1)}, bf16[352,2048]{1,0:T(8,128)(2,1)S(1)}, u32[]{:S(2)}, u32[]{:S(2)}) %collective-permute-start.4) | collective-permute-done | bytes 1441824 | tf_op jit(solution)/shard_map/ppermute | solution.py:484
  137.5 31.0 %collective-permute-done.5.refs_9_.refs_11_ = bf16[352,2048]{1,0:T(8,128)(2,1)} collective-permute-done((bf16[352,2048]{1,0:T(8,128)(2,1)}, bf16[352,2048]{1,0:T(8,128)(2,1)}, u32[]{:S(2)}, u32[]{:S(2)}) %collective-permute-start.5) | collective-permute-done | bytes 1441824 | tf_op jit(solution)/shard_map/ppermute | solution.py:484
  168.5 30.9 %collective-permute-done.3.refs_7_.refs_9_ = bf16[352,2048]{1,0:T(8,128)(2,1)} collective-permute-done((bf16[352,2048]{1,0:T(8,128)(2,1)}, bf16[352,2048]{1,0:T(8,128)(2,1)}, u32[]{:S(2)}, u32[]{:S(2)}) %collective-permute-start.3) | collective-permute-done | bytes 1441824 | tf_op jit(solution)/shard_map/ppermute | solution.py:484
  199.4 13.6 %experts.2 = bf16[32,16,2048]{2,1,0:T(8,128)(2,1)} custom-call(bf16[32,16,2048]{2,1,0:T(8,128)(2,1)} %copy-done.14, bf16[2,352,2048]{2,1,0:T(8,128)(2,1)} %bitcast.34, bf16[2,352,2048]{2,1,0:T(8,128)(2,1)} %bitcast.37, bf16[2,352,2048]{2,1,0:T(8,128)(2,1)} %refs_5_.1, bf16[352,2048]{1,0:T(8,128)(2,1)} %collective-permute-done.refs_4_.refs_6_, ...), custom_call_target="tpu_custom_call" | custom-call | flops 4429185024 | bytes 21495808 | tf_op jit(solution)/shard_map/experts/pallas_call | solution.py:366
  213.0 8.4 %all-to-all-start.4 = ((bf16[32,16,2048]{2,1,0:T(8,128)(2,1)}), bf16[32,16,2048]{2,1,0:T(8,128)(2,1)}, u32[]{:S(2)}, u32[]{:S(2)}) async-start(bf16[32,16,2048]{2,1,0:T(8,128)(2,1)} %experts.2), calls=%async_computation.4 | async-start | bytes 4194304 | tf_op jit(solution)/shard_map/all_to_all | solution.py:527
  228.4 20.6 %collective-permute-done.6.refs_1_ = bf16[32,8,2048]{2,1,0:T(8,128)(2,1)S(1)} collective-permute-done((bf16[32,8,2048]{2,1,0:T(8,128)(2,1)S(1)}, bf16[32,8,2048]{2,1,0:T(8,128)(2,1)S(1)}, u32[]{:S(2)}, u32[]{:S(2)}) %collective-permute-start.6) | collective-permute-done | bytes 1048608 | tf_op jit(solution)/shard_map/ppermute | solution.py:524
  249.0 13.8 %experts.3 = (bf16[32,16,2048]{2,1,0:T(8,128)(2,1)S(1)}, bf16[32,16,2048]{2,1,0:T(8,128)(2,1)S(1)}, bf16[2,3,704,2048]{3,2,1,0:T(8,128)(2,1)S(1)}) custom-call(bf16[32,16,2048]{2,1,0:T(8,128)(2,1)S(1)} %all-to-all-done.5.refs_0_, bf16[32,8,2048]{2,1,0:T(8,128)(2,1)S(1)} %collective-permute-done.6.refs_1_, ...), custom_call_target="tpu_custom_call" | custom-call | flops 8858370048 | bytes 25690112 | tf_op jit(solution)/shard_map/experts/pallas_call | solution.py:366
  262.8 6.0 %copy-done = bf16[2,3,704,2048]{3,2,1,0:T(8,128)(2,1)} copy-done((bf16[2,3,704,2048]{3,2,1,0:T(8,128)(2,1)}, bf16[2,3,704,2048]{3,2,1,0:T(8,128)(2,1)S(1)}, u32[]{:S(2)}) %copy-start) | copy-done | bytes 17301528
  271.6 9.0 %all-to-all-start.6 = ((bf16[32,16,2048]{2,1,0:T(8,128)(2,1)}), bf16[32,16,2048]{2,1,0:T(8,128)(2,1)S(1)}, u32[]{:S(2)}, u32[]{:S(2)}) async-start(bf16[32,16,2048]{2,1,0:T(8,128)(2,1)} %copy-done.6), calls=%async_computation.6 | async-start | bytes 4194304 | tf_op jit(solution)/shard_map/all_to_all | solution.py:527
  280.6 5.9 %copy-done.1 = bf16[2,3,704,2048]{3,2,1,0:T(8,128)(2,1)S(1)} copy-done((bf16[2,3,704,2048]{3,2,1,0:T(8,128)(2,1)S(1)}, bf16[2,3,704,2048]{3,2,1,0:T(8,128)(2,1)}, u32[]{:S(2)}) %copy-start.1) | copy-done | bytes 17301528
  286.5 7.9 %last_experts.1 = (bf16[256,2048]{1,0:T(8,128)(2,1)S(1)}, bf16[256,2048]{1,0:T(8,128)(2,1)S(1)}) custom-call(bf16[32,8,2048]{2,1,0:T(8,128)(2,1)S(1)} %collective-permute-done.12.xa, bf16[32,8,2048]{2,1,0:T(8,128)(2,1)} %collective-permute-done.13.xb, bf16[2,3,704,2048]{3,2,1,0:T(8,128)(2,1)S(1)} %copy-done.1), custom_call_target="tpu_custom_call" | custom-call | flops 4429185024 | bytes 4194304 | tf_op jit(solution)/shard_map/last_experts/pallas_call | solution.py:388
  296.3 23.9 %collective-permute-done.14.came_a = bf16[256,2048]{1,0:T(8,128)(2,1)S(1)} collective-permute-done((bf16[256,2048]{1,0:T(8,128)(2,1)S(1)}, bf16[256,2048]{1,0:T(8,128)(2,1)S(1)}, u32[]{:S(2)}, u32[]{:S(2)}) %collective-permute-start.14) | collective-permute-done | bytes 1048608 | tf_op jit(solution)/shard_map/ppermute | solution.py:554
  322.5 8.6 %all-to-all-start.7 = ((bf16[32,16,2048]{2,1,0:T(8,128)(2,1)}), bf16[32,16,2048]{2,1,0:T(8,128)(2,1)}, u32[]{:S(2)}, u32[]{:S(2)}) async-start(bf16[32,16,2048]{2,1,0:T(8,128)(2,1)} %merge.1), calls=%async_computation.7 | async-start | bytes 4194304 | tf_op jit(solution)/shard_map/all_to_all | solution.py:527
  332.4 3.5 collective-permute-done.8.mix_a
  340.8 9.9 %collective-permute-done.10 = bf16[128,2048]{1,0:T(8,128)(2,1)S(1)} collective-permute-done((bf16[128,2048]{1,0:T(8,128)(2,1)S(1)}, bf16[128,2048]{1,0:T(8,128)(2,1)S(1)}, u32[]{:S(2)}, u32[]{:S(2)}) %collective-permute-start.10) | collective-permute-done | bytes 524320 | tf_op jit(solution)/shard_map/ppermute | solution.py:548
  350.7 8.7 %all-to-all-done.7 = bf16[32,16,2048]{2,1,0:T(8,128)(2,1)} async-done(((bf16[32,16,2048]{2,1,0:T(8,128)(2,1)}), bf16[32,16,2048]{2,1,0:T(8,128)(2,1)}, u32[]{:S(2)}, u32[]{:S(2)}) %all-to-all-start.7) | async-done | bytes 2097184 | tf_op jit(solution)/shard_map/all_to_all | solution.py:527
  359.5 2.9 add_convert_fusion
  (79 shorter events, 30.3 us)
Async XLA Ops:
  24.6 12.2 %all-to-all-start.1 = ((bf16[32,24,128]{2,1,0:T(8,128)(2,1)}), bf16[32,24,128]{2,1,0:T(8,128)(2,1)S(1)}, u32[]{:S(2)}, u32[]{:S(2)}) async-start(bf16[32,24,128]{2,1,0:T(8,128)(2,1)} %prior_states.1), calls=%async_computation.1 | async-start | bytes 393216 | tf_op jit(solution)/shard_map/all_to_all | solution.py:497
  41.4 13.3 %copy-start.17 = (bf16[128,2048]{1,0:T(8,128)(2,1)S(1)}, bf16[128,2048]{1,0:T(8,128)(2,1)}, u32[]{:S(2)}) copy-start(bf16[128,2048]{1,0:T(8,128)(2,1)} %param.16) | copy-start | bytes 1572868
  41.4 13.3 %all-to-all-start.2 = ((bf16[4,128,512]{2,1,0:T(8,128)(2,1)}), bf16[4,128,512]{2,1,0:T(8,128)(2,1)S(1)}, u32[]{:S(2)}, u32[]{:S(2)}) async-start(bf16[4,128,512]{2,1,0:T(8,128)(2,1)} %outer_attention.1), calls=%async_computation.2 | async-start | bytes 1048576 | tf_op jit(solution)/shard_map/all_to_all | solution.py:503
  62.6 34.8 %all-to-all-start.3 = ((bf16[32,16,2048]{2,1,0:T(8,128)(2,1)}), bf16[32,16,2048]{2,1,0:T(8,128)(2,1)S(1)}, u32[]{:S(2)}, u32[]{:S(2)}) async-start(bf16[32,16,2048]{2,1,0:T(8,128)(2,1)} %bitcast.41), calls=%async_computation.3 | async-start | bytes 4194304 | tf_op jit(solution)/shard_map/all_to_all | solution.py:518
  69.1 37.8 %collective-permute-start.1 = (bf16[352,2048]{1,0:T(8,128)(2,1)}, bf16[352,2048]{1,0:T(8,128)(2,1)S(1)}, u32[]{:S(2)}, u32[]{:S(2)}) collective-permute-start(bf16[352,2048]{1,0:T(8,128)(2,1)} %get-tuple-element.28), channel_id=1, source_target_pairs={{0,1},{1,0},{2,3},{3,2},{4,5},{5,4},{6,7},{7,6},{8,9},{9,8},{10,11... | collective-permute-start | bytes 4325384 | tf_op jit(solution)/shard_map/ppermute | solution.py:484
  98.8 114.3 %all-to-all-start.5 = ((bf16[32,16,2048]{2,1,0:T(8,128)(2,1)}), bf16[32,16,2048]{2,1,0:T(8,128)(2,1)S(1)}, u32[]{:S(2)}, u32[]{:S(2)}) async-start(bf16[32,16,2048]{2,1,0:T(8,128)(2,1)} %bitcast.40), calls=%async_computation.5 | async-start | bytes 4194304 | tf_op jit(solution)/shard_map/all_to_all | solution.py:518
  103.2 34.3 %collective-permute-start.4 = (bf16[352,2048]{1,0:T(8,128)(2,1)}, bf16[352,2048]{1,0:T(8,128)(2,1)S(1)}, u32[]{:S(2)}, u32[]{:S(2)}) collective-permute-start(bf16[352,2048]{1,0:T(8,128)(2,1)} %get-tuple-element.31), channel_id=1, source_target_pairs={{0,3},{3,0},{1,2},{2,1},{4,7},{7,4},{5,6},{6,5},{8,11},{11,8},{9,1... | collective-permute-start | bytes 4325384 | tf_op jit(solution)/shard_map/ppermute | solution.py:484
  104.2 33.3 %collective-permute-start.2 = (bf16[352,2048]{1,0:T(8,128)(2,1)}, bf16[352,2048]{1,0:T(8,128)(2,1)}, u32[]{:S(2)}, u32[]{:S(2)}) collective-permute-start(bf16[352,2048]{1,0:T(8,128)(2,1)} %get-tuple-element.29), channel_id=1, source_target_pairs={{0,1},{1,0},{2,3},{3,2},{4,5},{5,4},{6,7},{7,6},{8,9},{9,8},{10,11... | collective-permute-start | bytes 4325384 | tf_op jit(solution)/shard_map/ppermute | solution.py:484
  104.2 64.3 %collective-permute-start.5 = (bf16[352,2048]{1,0:T(8,128)(2,1)}, bf16[352,2048]{1,0:T(8,128)(2,1)}, u32[]{:S(2)}, u32[]{:S(2)}) collective-permute-start(bf16[352,2048]{1,0:T(8,128)(2,1)} %get-tuple-element.32), channel_id=1, source_target_pairs={{0,3},{3,0},{1,2},{2,1},{4,7},{7,4},{5,6},{6,5},{8,11},{11,8},{9,1... | collective-permute-start | bytes 4325384 | tf_op jit(solution)/shard_map/ppermute | solution.py:484
  106.0 62.5 %collective-permute-start = (bf16[352,2048]{1,0:T(8,128)(2,1)}, bf16[352,2048]{1,0:T(8,128)(2,1)}, u32[]{:S(2)}, u32[]{:S(2)}) collective-permute-start(bf16[352,2048]{1,0:T(8,128)(2,1)} %get-tuple-element.27), channel_id=1, source_target_pairs={{0,1},{1,0},{2,3},{3,2},{4,5},{5,4},{6,7},{7,6},{8,9},{9,8},{10,11... | collective-permute-start | bytes 4325384 | tf_op jit(solution)/shard_map/ppermute | solution.py:484
  106.9 92.6 %copy-start.7 = (bf16[352,2048]{1,0:T(8,128)(2,1)}, bf16[352,2048]{1,0:T(8,128)(2,1)S(1)}, u32[]{:S(2)}) copy-start(bf16[352,2048]{1,0:T(8,128)(2,1)S(1)} %collective-permute-done.1.refs_5_.refs_7_) | copy-start | bytes 4325380
  106.9 92.6 %collective-permute-start.3 = (bf16[352,2048]{1,0:T(8,128)(2,1)}, bf16[352,2048]{1,0:T(8,128)(2,1)}, u32[]{:S(2)}, u32[]{:S(2)}) collective-permute-start(bf16[352,2048]{1,0:T(8,128)(2,1)} %get-tuple-element.30), channel_id=1, source_target_pairs={{0,3},{3,0},{1,2},{2,1},{4,7},{7,4},{5,6},{6,5},{8,11},{11,8},{9,1... | collective-permute-start | bytes 4325384 | tf_op jit(solution)/shard_map/ppermute | solution.py:484
  137.5 61.9 %copy-start.9 = (bf16[352,2048]{1,0:T(8,128)(2,1)}, bf16[352,2048]{1,0:T(8,128)(2,1)S(1)}, u32[]{:S(2)}) copy-start(bf16[352,2048]{1,0:T(8,128)(2,1)S(1)} %collective-permute-done.4.refs_8_.refs_10_) | copy-start | bytes 4325380
  213.0 58.5 %all-to-all-start.4 = ((bf16[32,16,2048]{2,1,0:T(8,128)(2,1)}), bf16[32,16,2048]{2,1,0:T(8,128)(2,1)}, u32[]{:S(2)}, u32[]{:S(2)}) async-start(bf16[32,16,2048]{2,1,0:T(8,128)(2,1)} %experts.2), calls=%async_computation.4 | async-start | bytes 4194304 | tf_op jit(solution)/shard_map/all_to_all | solution.py:527
  221.4 27.6 %copy-start.8 = (bf16[352,2048]{1,0:T(8,128)(2,1)S(1)}, bf16[352,2048]{1,0:T(8,128)(2,1)}, u32[]{:S(2)}) copy-start(bf16[352,2048]{1,0:T(8,128)(2,1)} %copy-done.7) | copy-start | bytes 4325380
  221.4 27.5 %copy-start.10 = (bf16[352,2048]{1,0:T(8,128)(2,1)S(1)}, bf16[352,2048]{1,0:T(8,128)(2,1)}, u32[]{:S(2)}) copy-start(bf16[352,2048]{1,0:T(8,128)(2,1)} %copy-done.9) | copy-start | bytes 4325380
  223.3 25.7 %collective-permute-start.6 = (bf16[32,8,2048]{2,1,0:T(8,128)(2,1)S(1)}, bf16[32,8,2048]{2,1,0:T(8,128)(2,1)S(1)}, u32[]{:S(2)}, u32[]{:S(2)}) collective-permute-start(bf16[32,8,2048]{2,1,0:T(8,128)(2,1)S(1)} %get-tuple-element.45), channel_id=1, source_target_pairs={{0,3},{3,0},{1,2},{2,1},{4,7},{7,4},{5,6},{6,5},{8,11},{11,8},{9,1... | collective-permute-start | bytes 3145736 | tf_op jit(solution)/shard_map/ppermute | solution.py:524
  224.2 24.7 %copy-start.2 = (bf16[2,2048,352]{1,2,0:T(8,128)(2,1)S(1)}, bf16[2,2048,352]{1,2,0:T(8,128)(2,1)}, u32[]{:S(2)}) copy-start(bf16[2,2048,352]{1,2,0:T(8,128)(2,1)} %param.21) | copy-start | bytes 8650756
  224.2 24.7 %collective-permute-start.7 = (bf16[32,8,2048]{2,1,0:T(8,128)(2,1)S(1)}, bf16[32,8,2048]{2,1,0:T(8,128)(2,1)S(1)}, u32[]{:S(2)}, u32[]{:S(2)}) collective-permute-start(bf16[32,8,2048]{2,1,0:T(8,128)(2,1)S(1)} %get-tuple-element.44), channel_id=1, source_target_pairs={{0,1},{1,0},{2,3},{3,2},{4,5},{5,4},{6,7},{7,6},{8,9},{9,8},{10,11... | collective-permute-start | bytes 3145736 | tf_op jit(solution)/shard_map/ppermute | solution.py:524
  225.7 54.9 %collective-permute-start.12 = (bf16[32,8,2048]{2,1,0:T(8,128)(2,1)}, bf16[32,8,2048]{2,1,0:T(8,128)(2,1)S(1)}, u32[]{:S(2)}, u32[]{:S(2)}) collective-permute-start(bf16[32,8,2048]{2,1,0:T(8,128)(2,1)} %get-tuple-element.43), channel_id=1, source_target_pairs={{0,3},{3,0},{1,2},{2,1},{4,7},{7,4},{5,6},{6,5},{8,11},{11,8},{9,1... | collective-permute-start | bytes 3145736 | tf_op jit(solution)/shard_map/ppermute | solution.py:524
  227.5 53.1 %collective-permute-start.13 = (bf16[32,8,2048]{2,1,0:T(8,128)(2,1)}, bf16[32,8,2048]{2,1,0:T(8,128)(2,1)}, u32[]{:S(2)}, u32[]{:S(2)}) collective-permute-start(bf16[32,8,2048]{2,1,0:T(8,128)(2,1)} %get-tuple-element.42), channel_id=1, source_target_pairs={{0,1},{1,0},{2,3},{3,2},{4,5},{5,4},{6,7},{7,6},{8,9},{9,8},{10,11... | collective-permute-start | bytes 3145736 | tf_op jit(solution)/shard_map/ppermute | solution.py:524
  271.6 51.0 %all-to-all-start.6 = ((bf16[32,16,2048]{2,1,0:T(8,128)(2,1)}), bf16[32,16,2048]{2,1,0:T(8,128)(2,1)S(1)}, u32[]{:S(2)}, u32[]{:S(2)}) async-start(bf16[32,16,2048]{2,1,0:T(8,128)(2,1)} %copy-done.6), calls=%async_computation.6 | async-start | bytes 4194304 | tf_op jit(solution)/shard_map/all_to_all | solution.py:527
  286.5 33.9 %copy-start.4 = (bf16[32,16,2048]{2,1,0:T(8,128)(2,1)S(1)}, bf16[32,16,2048]{2,1,0:T(8,128)(2,1)}, u32[]{:S(2)}) copy-start(bf16[32,16,2048]{2,1,0:T(8,128)(2,1)} %copy-done.3) | copy-start | bytes 6291460
  294.4 25.8 %collective-permute-start.14 = (bf16[256,2048]{1,0:T(8,128)(2,1)S(1)}, bf16[256,2048]{1,0:T(8,128)(2,1)S(1)}, u32[]{:S(2)}, u32[]{:S(2)}) collective-permute-start(bf16[256,2048]{1,0:T(8,128)(2,1)S(1)} %get-tuple-element.40), channel_id=1, source_target_pairs={{0,3},{3,0},{1,2},{2,1},{4,7},{7,4},{5,6},{6,5},{8,11},{11,8},{9,1... | collective-permute-start | bytes 3145736 | tf_op jit(solution)/shard_map/ppermute | solution.py:554
  296.2 24.2 %collective-permute-start.15 = (bf16[256,2048]{1,0:T(8,128)(2,1)S(1)}, bf16[256,2048]{1,0:T(8,128)(2,1)S(1)}, u32[]{:S(2)}, u32[]{:S(2)}) collective-permute-start(bf16[256,2048]{1,0:T(8,128)(2,1)S(1)} %get-tuple-element.41), channel_id=1, source_target_pairs={{0,1},{1,0},{2,3},{3,2},{4,5},{5,4},{6,7},{7,6},{8,9},{9,8},{10,11... | collective-permute-start | bytes 3145736 | tf_op jit(solution)/shard_map/ppermute | solution.py:554
  322.5 8.6 %copy-start.22 = (bf16[256,128]{1,0:T(8,128)(2,1)S(1)}, bf16[256,128]{1,0:T(8,128)(2,1)}, u32[]{:S(2)}) copy-start(bf16[256,128]{1,0:T(8,128)(2,1)} %get-tuple-element.34) | copy-start | bytes 196612
  322.5 9.9 %copy-start.21 = (bf16[256,128]{1,0:T(8,128)(2,1)S(1)}, bf16[256,128]{1,0:T(8,128)(2,1)}, u32[]{:S(2)}) copy-start(bf16[256,128]{1,0:T(8,128)(2,1)} %get-tuple-element.35) | copy-start | bytes 196612
  322.5 37.0 %all-to-all-start.7 = ((bf16[32,16,2048]{2,1,0:T(8,128)(2,1)}), bf16[32,16,2048]{2,1,0:T(8,128)(2,1)}, u32[]{:S(2)}, u32[]{:S(2)}) async-start(bf16[32,16,2048]{2,1,0:T(8,128)(2,1)} %merge.1), calls=%async_computation.7 | async-start | bytes 4194304 | tf_op jit(solution)/shard_map/all_to_all | solution.py:527
  331.1 4.8 %collective-permute-start.8 = (bf16[256,128]{1,0:T(8,128)(2,1)S(1)}, bf16[256,128]{1,0:T(8,128)(2,1)S(1)}, u32[]{:S(2)}, u32[]{:S(2)}) collective-permute-start(bf16[256,128]{1,0:T(8,128)(2,1)S(1)} %copy-done.22), channel_id=1, source_target_pairs={{0,3},{3,0},{1,2},{2,1},{4,7},{7,4},{5,6},{6,5},{8,11},{11,8},{9,1... | collective-permute-start | bytes 196616 | tf_op jit(solution)/shard_map/ppermute | solution.py:494
  332.4 3.5 collective-permute-start.9
  337.2 13.5 %collective-permute-start.10 = (bf16[128,2048]{1,0:T(8,128)(2,1)S(1)}, bf16[128,2048]{1,0:T(8,128)(2,1)S(1)}, u32[]{:S(2)}, u32[]{:S(2)}) collective-permute-start(bf16[128,2048]{1,0:T(8,128)(2,1)S(1)} %get-tuple-element.36), channel_id=1, source_target_pairs={{0,3},{3,0},{1,2},{2,1},{4,7},{7,4},{5,6},{6,5},{8,11},{11,8},{9,1... | collective-permute-start | bytes 1572872 | tf_op jit(solution)/shard_map/ppermute | solution.py:548
  338.7 12.0 %collective-permute-start.11 = (bf16[128,2048]{1,0:T(8,128)(2,1)S(1)}, bf16[128,2048]{1,0:T(8,128)(2,1)S(1)}, u32[]{:S(2)}, u32[]{:S(2)}) collective-permute-start(bf16[128,2048]{1,0:T(8,128)(2,1)S(1)} %get-tuple-element.37), channel_id=1, source_target_pairs={{0,1},{1,0},{2,3},{3,2},{4,5},{5,4},{6,7},{7,6},{8,9},{9,8},{10,11... | collective-permute-start | bytes 1572872 | tf_op jit(solution)/shard_map/ppermute | solution.py:549
  (14 other events, 62.5 us)

commit v3 on v2

--- a/solution.py
+++ b/solution.py
@@ -17,6 +17,7 @@
 EXTRA = 8
 GRANT = 58 << 20
 KEEP_GRANT = 16 << 20
+MIDDLE_GRANT = 36 << 20
 FAR = [(0, 3), (3, 0), (1, 2), (2, 1)]
 NEAR = [(0, 1), (1, 0), (2, 3), (3, 2)]
 F32 = jnp.float32
@@ -368,28 +369,45 @@
         out_shape=out_shape + [held] if keep else out_shape,
         in_specs=[anywhere] * (len(xs) + 9),
         scratch_shapes=scratch if keep else [held] + scratch,
-        compiler_params=pltpu.CompilerParams(vmem_limit_bytes=KEEP_GRANT if keep else GRANT),
+        compiler_params=pltpu.CompilerParams(vmem_limit_bytes=MIDDLE_GRANT if keep else GRANT),
         cost_estimate=expert_cost(2 * blocks * rows * len(sets), quarter, 1),
         name="experts",
     )(*xs, *own, *fars[0], *fars[1])
 
 
-def last_body(xa, xb, weights, out_a, out_b):
+def last_body(xa, xb, weights, out_a, out_b, xs, ys, sems):
+    loads, stores = [], []
     for e, (x_ref, out) in enumerate(((xa, out_a), (xb, out_b))):
-
-        def emit(cols, part, out=out):
-            out[:, cols] = part
-
-        expert_rows(x_ref[...].reshape(-1, D), weights, e, lambda i: None, emit)
+        loads.append(pltpu.make_async_copy(x_ref, xs.at[e], sems.at[e]))
+        stores.append(pltpu.make_async_copy(ys.at[e], out, sems.at[2 + e]))
+        loads[e].start()
+    for e in range(2):
+
+        def emit(cols, part, e=e):
+            ys[e, :, cols] = part
+
+        loads[e].wait()
+        expert_rows(xs[e].reshape(-1, D), weights, e, lambda i: None, emit)
+        stores[e].start()
+    for store in stores:
+        store.wait()
 
 
 def last_experts(xa, xb, weights):
     blocks, rows, _ = xa.shape
+    total = blocks * rows
     return pl.pallas_call(
         last_body,
-        out_shape=[jax.ShapeDtypeStruct((blocks * rows, D), BF16)] * 2,
+        out_shape=[jax.ShapeDtypeStruct((total, D), BF16)] * 2,
+        in_specs=[ANYWHERE, ANYWHERE, ON_CHIP],
+        out_specs=[ANYWHERE, ANYWHERE],
+        scratch_shapes=[
+            pltpu.VMEM((2, blocks, rows, D), BF16),
+            pltpu.VMEM((2, total, D), BF16),
+            pltpu.SemaphoreType.DMA((4,)),
+        ],
         compiler_params=pltpu.CompilerParams(vmem_limit_bytes=KEEP_GRANT),
-        cost_estimate=expert_cost(2 * blocks * rows, weights.shape[2] // 2, 0),
+        cost_estimate=expert_cost(2 * total, weights.shape[2] // 2, 0),
         name="last_experts",
     )(xa, xb, weights)
 

time: 364 us -> 361 us (level)
    unnamed x46 -> x44, local copies, waits for them, and re-layouts: 19 us -> 16.5 us
where the time goes in v3:
time: 361 us; the launch traced here: 360 us
  waiting for transfers between devices  189 us (52%)
  Pallas kernels  59.8 us (17%)
  starting transfers between devices  59 us (16%)
  local copies, waits for them, and re-layouts  19.7 us (5%)
  blocking collectives  17.7 us (5%)
  matrix products  14.1 us (4%)
    ppermute x6, waiting for transfers between devices, send(): far.append(lax.ppermute(parts[which], 'grp', pairs[which][0]))  91.6 us
    pallas_call x2, Pallas kernels, experts(): pl.pallas_call(functools.partial(experts_body, sets), out_shape=out_shape...  29.7 us
    all_to_all x3, starting transfers between devices, home(): return lax.all_to_all(rows, 'ctx', 0, 0, tiled=True)  26.1 us
    all_to_all x2, waiting for transfers between devices, on_device(): lax.all_to_all(buffer.reshape(n_ctx, 2 * half, D), 'ctx', 0, 0, tiled=True)  25.8 us
    ppermute x2, waiting for transfers between devices, on_device(): came.append(lax.ppermute(results[which], 'grp', pairs[which][1]))  24.2 us
    ppermute x4, waiting for transfers between devices, on_device(): others.append(lax.ppermute(own, 'grp', pairs[which][1]))  19.1 us
    all_to_all x1, blocking collectives, on_device(): got = lax.all_to_all(payload, 'ctx', 0, 0, tiled=True)  17.7 us
    unnamed x44, local copies, waits for them, and re-layouts  16.5 us
  transfers between devices with their start and end apart: 23, of which 12 were waited for; matrix products, arithmetic and copies ran while one was open for 2% of the time, Pallas kernels for 14%

profile of v3, /device:TPU:1, one launch (start us, length us, event | category | flops | bytes accessed | tf_op | source)
XLA Modules:
  0.0 360.3 jit_solution(10503085833243310183)
XLA Ops:
  0.6 5.3 %local_states.1 = (bf16[32,24,128]{2,1,0:T(8,128)(2,1)}, bf16[352,2048]{1,0:T(8,128)(2,1)}, bf16[352,2048]{1,0:T(8,128)(2,1)}) custom-call(bf16[512,512]{1,0:T(8,128)(2,1)} %k_ref.3, bf16[512,512]{1,0:T(8,128)(2,1)} %v_ref.3, f32[4,512]{1,0:T(4,128)} %decay_ref.5, bf16[2,352,2048]{2,1,0:T(8,128)(2,1)} %bitcast.36), custom_call_target="tpu_custom_call" | custom-call | tf_op jit(solution)/shard_map/local_states/pallas_call | solution.py:107
  6.0 17.7 %all_to_all.40.got_ref = bf16[32,24,128]{2,1,0:T(8,128)(2,1)S(1)} all-to-all(bf16[32,24,128]{2,1,0:T(8,128)(2,1)} %get-tuple-element.22), channel_id=1, replica_groups=mesh['ctx'=32,'grp'=4] {'ctx'}, dimensions={0} | all-to-all | bytes 393216 | tf_op jit(solution)/shard_map/all_to_all | solution.py:508
  24.7 3.8 %all-to-all-start.1 = ((bf16[32,24,128]{2,1,0:T(8,128)(2,1)}), bf16[32,24,128]{2,1,0:T(8,128)(2,1)S(1)}, u32[]{:S(2)}, u32[]{:S(2)}) async-start(bf16[32,24,128]{2,1,0:T(8,128)(2,1)} %prior_states.1), calls=%async_computation.1 | async-start | bytes 393216 | tf_op jit(solution)/shard_map/all_to_all | solution.py:515
  28.5 6.3 %inner_attention.1 = (f32[512,512]{1,0:T(8,128)}, f32[512,128]{1,0:T(8,128)}, bf16[352,2048]{1,0:T(8,128)(2,1)}, bf16[352,2048]{1,0:T(8,128)(2,1)}) custom-call(bf16[512,512]{1,0:T(8,128)(2,1)} %q_ref.3, bf16[512,512]{1,0:T(8,128)(2,1)} %k_ref.3, bf16[512,512]{1,0:T(8,128)(2,1)} %v_ref.3, f32[4,512]{1,0:T(4,128)} %decay_ref.5, bf16[2,352,2048]{2,1,0:T(8,128)(2,1)} %bitcast.33), custom_call_target="tpu_custom_call" | custom-call | flops 536870912 | bytes 2097152 | tf_op jit(solution)/shard_map/inner_attention/pallas_call | solution.py:187
  39.1 2.4 outer_attention.1
  41.5 4.3 %all-to-all-start.2 = ((bf16[4,128,512]{2,1,0:T(8,128)(2,1)}), bf16[4,128,512]{2,1,0:T(8,128)(2,1)S(1)}, u32[]{:S(2)}, u32[]{:S(2)}) async-start(bf16[4,128,512]{2,1,0:T(8,128)(2,1)} %outer_attention.1), calls=%async_computation.2 | async-start | bytes 1048576 | tf_op jit(solution)/shard_map/all_to_all | solution.py:521
  45.8 4.9 %route.1 = (bf16[2,512,128]{2,1,0:T(8,128)(2,1)}, bf16[2,512,128]{2,1,0:T(8,128)(2,1)}, bf16[256,128]{1,0:T(8,128)(2,1)}, bf16[256,128]{1,0:T(8,128)(2,1)}, bf16...) custom-call(s32[6,128]{1,0:T(8,128)} %bitcast.42, f32[6,128]{1,0:T(8,128)} %bitcast.43, bf16[2,352,2048]{2,1,0:T(8,128)(2,1)} %refs_5_.1), custom_call_target="tpu_custom_call" | custom-call | tf_op jit(solution)/shard_map/route/pallas_call | solution.py:274
  50.7 4.0 %all-to-all-done.2 = bf16[4,128,512]{2,1,0:T(8,128)(2,1)S(1)} async-done(((bf16[4,128,512]{2,1,0:T(8,128)(2,1)}), bf16[4,128,512]{2,1,0:T(8,128)(2,1)S(1)}, u32[]{:S(2)}, u32[]{:S(2)}) %all-to-all-start.2) | async-done | bytes 524320 | tf_op jit(solution)/shard_map/all_to_all | solution.py:521
  54.8 4.8 %fusion.2 = (f32[128]{0:T(128)S(1)}, bf16[128,2048]{1,0:T(8,128)(2,1)S(1)}) fusion(bf16[4,128,512]{2,1,0:T(8,128)(2,1)S(1)} %all-to-all-done.2, bf16[4,512,2048]{2,1,0:T(8,128)(2,1)} %bitcast.39, bf16[128,2048]{1,0:T(8,128)(2,1)S(1)} %copy-done.15), kind=kOutput, calls=%fused_computation.8 | convolution fusion | flops 1075314560 | bytes 9961984 | tf_op jit(solution)/shard_map/gtc,gcd->td/dot_general | solution.py:522
  59.7 2.1 convolution_convert_fusion.1
  61.8 6.5 %all-to-all-start.3 = ((bf16[32,16,2048]{2,1,0:T(8,128)(2,1)}), bf16[32,16,2048]{2,1,0:T(8,128)(2,1)S(1)}, u32[]{:S(2)}, u32[]{:S(2)}) async-start(bf16[32,16,2048]{2,1,0:T(8,128)(2,1)} %bitcast.41), calls=%async_computation.3 | async-start | bytes 4194304 | tf_op jit(solution)/shard_map/all_to_all | solution.py:536
  68.7 2.2 convolution_convert_fusion
  70.8 25.8 %all-to-all-done.3.refs_0_ = bf16[32,16,2048]{2,1,0:T(8,128)(2,1)S(1)} async-done(((bf16[32,16,2048]{2,1,0:T(8,128)(2,1)}), bf16[32,16,2048]{2,1,0:T(8,128)(2,1)S(1)}, u32[]{:S(2)}, u32[]{:S(2)}) %all-to-all-start.3) | async-done | bytes 2097184 | tf_op jit(solution)/shard_map/all_to_all | solution.py:536
  98.0 5.2 %all-to-all-start.5 = ((bf16[32,16,2048]{2,1,0:T(8,128)(2,1)}), bf16[32,16,2048]{2,1,0:T(8,128)(2,1)}, u32[]{:S(2)}, u32[]{:S(2)}) async-start(bf16[32,16,2048]{2,1,0:T(8,128)(2,1)} %bitcast.40), calls=%async_computation.5 | async-start | bytes 4194304 | tf_op jit(solution)/shard_map/all_to_all | solution.py:536
  107.7 29.7 %collective-permute-done.4.refs_8_.refs_10_ = bf16[352,2048]{1,0:T(8,128)(2,1)S(1)} collective-permute-done((bf16[352,2048]{1,0:T(8,128)(2,1)}, bf16[352,2048]{1,0:T(8,128)(2,1)S(1)}, u32[]{:S(2)}, u32[]{:S(2)}) %collective-permute-start.4) | collective-permute-done | bytes 1441824 | tf_op jit(solution)/shard_map/ppermute | solution.py:502
  137.4 30.9 %collective-permute-done.5.refs_9_.refs_11_ = bf16[352,2048]{1,0:T(8,128)(2,1)S(1)} collective-permute-done((bf16[352,2048]{1,0:T(8,128)(2,1)}, bf16[352,2048]{1,0:T(8,128)(2,1)S(1)}, u32[]{:S(2)}, u32[]{:S(2)}) %collective-permute-start.5) | collective-permute-done | bytes 1441824 | tf_op jit(solution)/shard_map/ppermute | solution.py:502
  168.3 31.0 %collective-permute-done.3.refs_7_.refs_9_ = bf16[352,2048]{1,0:T(8,128)(2,1)} collective-permute-done((bf16[352,2048]{1,0:T(8,128)(2,1)}, bf16[352,2048]{1,0:T(8,128)(2,1)}, u32[]{:S(2)}, u32[]{:S(2)}) %collective-permute-start.3) | collective-permute-done | bytes 1441824 | tf_op jit(solution)/shard_map/ppermute | solution.py:502
  199.3 13.6 %experts.2 = bf16[32,16,2048]{2,1,0:T(8,128)(2,1)} custom-call(bf16[32,16,2048]{2,1,0:T(8,128)(2,1)} %copy-done.7, bf16[2,352,2048]{2,1,0:T(8,128)(2,1)} %bitcast.37, bf16[2,352,2048]{2,1,0:T(8,128)(2,1)} %bitcast.34, bf16[2,352,2048]{2,1,0:T(8,128)(2,1)} %refs_5_.1, bf16[352,2048]{1,0:T(8,128)(2,1)} %copy-done.14, ...), custom_call_target="tpu_custom_call" | custom-call | flops 4429185024 | bytes 21495808 | tf_op jit(solution)/shard_map/experts/pallas_call | solution.py:367
  212.9 8.6 %all-to-all-start.4 = ((bf16[32,16,2048]{2,1,0:T(8,128)(2,1)}), bf16[32,16,2048]{2,1,0:T(8,128)(2,1)}, u32[]{:S(2)}, u32[]{:S(2)}) async-start(bf16[32,16,2048]{2,1,0:T(8,128)(2,1)} %experts.2), calls=%async_computation.4 | async-start | bytes 4194304 | tf_op jit(solution)/shard_map/all_to_all | solution.py:545
  222.7 3.1 fusion.18
  228.4 19.1 %collective-permute-done.6.refs_1_ = bf16[32,8,2048]{2,1,0:T(8,128)(2,1)S(1)} collective-permute-done((bf16[32,8,2048]{2,1,0:T(8,128)(2,1)S(1)}, bf16[32,8,2048]{2,1,0:T(8,128)(2,1)S(1)}, u32[]{:S(2)}, u32[]{:S(2)}) %collective-permute-start.6) | collective-permute-done | bytes 1048608 | tf_op jit(solution)/shard_map/ppermute | solution.py:542
  248.5 16.2 %experts.3 = (bf16[32,16,2048]{2,1,0:T(8,128)(2,1)}, bf16[32,16,2048]{2,1,0:T(8,128)(2,1)}, bf16[2,3,704,2048]{3,2,1,0:T(8,128)(2,1)S(1)}) custom-call(bf16[32,16,2048]{2,1,0:T(8,128)(2,1)} %all-to-all-done.5.refs_0_, bf16[32,8,2048]{2,1,0:T(8,128)(2,1)S(1)} %collective-permute-done.6.refs_1_, bf16[32,8,2048]{2,1,0:T(8,128)(2,1)} %copy-done.19, ...), custom_call_target="tpu_custom_call" | custom-call | flops 8858370048 | bytes 25690112 | tf_op jit(solution)/shard_map/experts/pallas_call | solution.py:367
  264.6 6.0 %copy-done = bf16[2,3,704,2048]{3,2,1,0:T(8,128)(2,1)} copy-done((bf16[2,3,704,2048]{3,2,1,0:T(8,128)(2,1)}, bf16[2,3,704,2048]{3,2,1,0:T(8,128)(2,1)S(1)}, u32[]{:S(2)}) %copy-start) | copy-done | bytes 17301528
  270.6 8.9 %all-to-all-start.6 = ((bf16[32,16,2048]{2,1,0:T(8,128)(2,1)}), bf16[32,16,2048]{2,1,0:T(8,128)(2,1)S(1)}, u32[]{:S(2)}, u32[]{:S(2)}) async-start(bf16[32,16,2048]{2,1,0:T(8,128)(2,1)} %get-tuple-element.33), calls=%async_computation.6 | async-start | bytes 4194304 | tf_op jit(solution)/shard_map/all_to_all | solution.py:545
  279.6 5.9 %copy-done.1 = bf16[2,3,704,2048]{3,2,1,0:T(8,128)(2,1)S(1)} copy-done((bf16[2,3,704,2048]{3,2,1,0:T(8,128)(2,1)S(1)}, bf16[2,3,704,2048]{3,2,1,0:T(8,128)(2,1)}, u32[]{:S(2)}) %copy-start.1) | copy-done | bytes 17301528
  285.5 6.8 %last_experts.1 = (bf16[256,2048]{1,0:T(8,128)(2,1)S(1)}, bf16[256,2048]{1,0:T(8,128)(2,1)S(1)}) custom-call(bf16[32,8,2048]{2,1,0:T(8,128)(2,1)S(1)} %collective-permute-done.12.xa, bf16[32,8,2048]{2,1,0:T(8,128)(2,1)} %collective-permute-done.13.xb, bf16[2,3,704,2048]{3,2,1,0:T(8,128)(2,1)S(1)} %copy-done.1), custom_call_target="tpu_custom_call" | custom-call | flops 4429185024 | bytes 4194304 | tf_op jit(solution)/shard_map/last_experts/pallas_call | solution.py:399
  294.1 23.9 %collective-permute-done.14.came_a = bf16[256,2048]{1,0:T(8,128)(2,1)S(1)} collective-permute-done((bf16[256,2048]{1,0:T(8,128)(2,1)S(1)}, bf16[256,2048]{1,0:T(8,128)(2,1)S(1)}, u32[]{:S(2)}, u32[]{:S(2)}) %collective-permute-start.14) | collective-permute-done | bytes 1048608 | tf_op jit(solution)/shard_map/ppermute | solution.py:572
  320.4 8.6 %all-to-all-start.7 = ((bf16[32,16,2048]{2,1,0:T(8,128)(2,1)}), bf16[32,16,2048]{2,1,0:T(8,128)(2,1)}, u32[]{:S(2)}, u32[]{:S(2)}) async-start(bf16[32,16,2048]{2,1,0:T(8,128)(2,1)} %merge.1), calls=%async_computation.7 | async-start | bytes 4194304 | tf_op jit(solution)/shard_map/all_to_all | solution.py:545
  330.3 3.5 collective-permute-done.8.mix_a
  338.7 9.9 %collective-permute-done.10 = bf16[128,2048]{1,0:T(8,128)(2,1)S(1)} collective-permute-done((bf16[128,2048]{1,0:T(8,128)(2,1)S(1)}, bf16[128,2048]{1,0:T(8,128)(2,1)S(1)}, u32[]{:S(2)}, u32[]{:S(2)}) %collective-permute-start.10) | collective-permute-done | bytes 524320 | tf_op jit(solution)/shard_map/ppermute | solution.py:566
  348.6 8.7 %all-to-all-done.7 = bf16[32,16,2048]{2,1,0:T(8,128)(2,1)} async-done(((bf16[32,16,2048]{2,1,0:T(8,128)(2,1)}), bf16[32,16,2048]{2,1,0:T(8,128)(2,1)}, u32[]{:S(2)}, u32[]{:S(2)}) %all-to-all-start.7) | async-done | bytes 2097184 | tf_op jit(solution)/shard_map/all_to_all | solution.py:545
  357.4 2.9 add_convert_fusion
  (77 shorter events, 26.7 us)
Async XLA Ops:
  24.7 12.2 %all-to-all-start.1 = ((bf16[32,24,128]{2,1,0:T(8,128)(2,1)}), bf16[32,24,128]{2,1,0:T(8,128)(2,1)S(1)}, u32[]{:S(2)}, u32[]{:S(2)}) async-start(bf16[32,24,128]{2,1,0:T(8,128)(2,1)} %prior_states.1), calls=%async_computation.1 | async-start | bytes 393216 | tf_op jit(solution)/shard_map/all_to_all | solution.py:515
  41.5 13.3 %copy-start.15 = (bf16[128,2048]{1,0:T(8,128)(2,1)S(1)}, bf16[128,2048]{1,0:T(8,128)(2,1)}, u32[]{:S(2)}) copy-start(bf16[128,2048]{1,0:T(8,128)(2,1)} %param.16) | copy-start | bytes 1572868
  41.5 13.3 %all-to-all-start.2 = ((bf16[4,128,512]{2,1,0:T(8,128)(2,1)}), bf16[4,128,512]{2,1,0:T(8,128)(2,1)S(1)}, u32[]{:S(2)}, u32[]{:S(2)}) async-start(bf16[4,128,512]{2,1,0:T(8,128)(2,1)} %outer_attention.1), calls=%async_computation.2 | async-start | bytes 1048576 | tf_op jit(solution)/shard_map/all_to_all | solution.py:521
  59.6 9.0 %copy-start.9 = (bf16[128,2048]{1,0:T(8,128)(2,1)}, bf16[128,2048]{1,0:T(8,128)(2,1)S(1)}, u32[]{:S(2)}) copy-start(bf16[128,2048]{1,0:T(8,128)(2,1)S(1)} %get-tuple-element.47) | copy-start | bytes 1572868
  61.8 34.8 %all-to-all-start.3 = ((bf16[32,16,2048]{2,1,0:T(8,128)(2,1)}), bf16[32,16,2048]{2,1,0:T(8,128)(2,1)S(1)}, u32[]{:S(2)}, u32[]{:S(2)}) async-start(bf16[32,16,2048]{2,1,0:T(8,128)(2,1)} %bitcast.41), calls=%async_computation.3 | async-start | bytes 4194304 | tf_op jit(solution)/shard_map/all_to_all | solution.py:536
  68.3 38.5 %collective-permute-start.1 = (bf16[352,2048]{1,0:T(8,128)(2,1)}, bf16[352,2048]{1,0:T(8,128)(2,1)}, u32[]{:S(2)}, u32[]{:S(2)}) collective-permute-start(bf16[352,2048]{1,0:T(8,128)(2,1)} %get-tuple-element.28), channel_id=1, source_target_pairs={{0,1},{1,0},{2,3},{3,2},{4,5},{5,4},{6,7},{7,6},{8,9},{9,8},{10,11... | collective-permute-start | bytes 4325384 | tf_op jit(solution)/shard_map/ppermute | solution.py:502
  98.0 114.9 %all-to-all-start.5 = ((bf16[32,16,2048]{2,1,0:T(8,128)(2,1)}), bf16[32,16,2048]{2,1,0:T(8,128)(2,1)}, u32[]{:S(2)}, u32[]{:S(2)}) async-start(bf16[32,16,2048]{2,1,0:T(8,128)(2,1)} %bitcast.40), calls=%async_computation.5 | async-start | bytes 4194304 | tf_op jit(solution)/shard_map/all_to_all | solution.py:536
  103.2 34.2 %collective-permute-start.4 = (bf16[352,2048]{1,0:T(8,128)(2,1)}, bf16[352,2048]{1,0:T(8,128)(2,1)S(1)}, u32[]{:S(2)}, u32[]{:S(2)}) collective-permute-start(bf16[352,2048]{1,0:T(8,128)(2,1)} %get-tuple-element.31), channel_id=1, source_target_pairs={{0,3},{3,0},{1,2},{2,1},{4,7},{7,4},{5,6},{6,5},{8,11},{11,8},{9,1... | collective-permute-start | bytes 4325384 | tf_op jit(solution)/shard_map/ppermute | solution.py:502
  104.2 33.3 %collective-permute-start.2 = (bf16[352,2048]{1,0:T(8,128)(2,1)}, bf16[352,2048]{1,0:T(8,128)(2,1)S(1)}, u32[]{:S(2)}, u32[]{:S(2)}) collective-permute-start(bf16[352,2048]{1,0:T(8,128)(2,1)} %get-tuple-element.29), channel_id=1, source_target_pairs={{0,1},{1,0},{2,3},{3,2},{4,5},{5,4},{6,7},{7,6},{8,9},{9,8},{10,11... | collective-permute-start | bytes 4325384 | tf_op jit(solution)/shard_map/ppermute | solution.py:502
  104.2 64.1 %collective-permute-start.5 = (bf16[352,2048]{1,0:T(8,128)(2,1)}, bf16[352,2048]{1,0:T(8,128)(2,1)S(1)}, u32[]{:S(2)}, u32[]{:S(2)}) collective-permute-start(bf16[352,2048]{1,0:T(8,128)(2,1)} %get-tuple-element.32), channel_id=1, source_target_pairs={{0,3},{3,0},{1,2},{2,1},{4,7},{7,4},{5,6},{6,5},{8,11},{11,8},{9,1... | collective-permute-start | bytes 4325384 | tf_op jit(solution)/shard_map/ppermute | solution.py:502
  106.0 62.4 %collective-permute-start = (bf16[352,2048]{1,0:T(8,128)(2,1)}, bf16[352,2048]{1,0:T(8,128)(2,1)S(1)}, u32[]{:S(2)}, u32[]{:S(2)}) collective-permute-start(bf16[352,2048]{1,0:T(8,128)(2,1)} %get-tuple-element.27), channel_id=1, source_target_pairs={{0,1},{1,0},{2,3},{3,2},{4,5},{5,4},{6,7},{7,6},{8,9},{9,8},{10,11... | collective-permute-start | bytes 4325384 | tf_op jit(solution)/shard_map/ppermute | solution.py:502
  106.8 92.5 %collective-permute-start.3 = (bf16[352,2048]{1,0:T(8,128)(2,1)}, bf16[352,2048]{1,0:T(8,128)(2,1)}, u32[]{:S(2)}, u32[]{:S(2)}) collective-permute-start(bf16[352,2048]{1,0:T(8,128)(2,1)} %get-tuple-element.30), channel_id=1, source_target_pairs={{0,3},{3,0},{1,2},{2,1},{4,7},{7,4},{5,6},{6,5},{8,11},{11,8},{9,1... | collective-permute-start | bytes 4325384 | tf_op jit(solution)/shard_map/ppermute | solution.py:502
  137.4 61.9 %copy-start.11 = (bf16[352,2048]{1,0:T(8,128)(2,1)}, bf16[352,2048]{1,0:T(8,128)(2,1)S(1)}, u32[]{:S(2)}) copy-start(bf16[352,2048]{1,0:T(8,128)(2,1)S(1)} %collective-permute-done.4.refs_8_.refs_10_) | copy-start | bytes 4325380
  137.4 61.9 %copy-start.12 = (bf16[352,2048]{1,0:T(8,128)(2,1)}, bf16[352,2048]{1,0:T(8,128)(2,1)S(1)}, u32[]{:S(2)}) copy-start(bf16[352,2048]{1,0:T(8,128)(2,1)S(1)} %collective-permute-done.2.refs_6_.refs_8_) | copy-start | bytes 4325380
  168.3 31.0 %copy-start.13 = (bf16[352,2048]{1,0:T(8,128)(2,1)}, bf16[352,2048]{1,0:T(8,128)(2,1)S(1)}, u32[]{:S(2)}) copy-start(bf16[352,2048]{1,0:T(8,128)(2,1)S(1)} %collective-permute-done.5.refs_9_.refs_11_) | copy-start | bytes 4325380
  168.3 31.0 %copy-start.14 = (bf16[352,2048]{1,0:T(8,128)(2,1)}, bf16[352,2048]{1,0:T(8,128)(2,1)S(1)}, u32[]{:S(2)}) copy-start(bf16[352,2048]{1,0:T(8,128)(2,1)S(1)} %collective-permute-done.refs_4_.refs_6_) | copy-start | bytes 4325380
  212.9 8.6 %copy-start.8 = (bf16[32,16,2048]{2,1,0:T(8,128)(2,1)S(1)}, bf16[32,16,2048]{2,1,0:T(8,128)(2,1)}, u32[]{:S(2)}) copy-start(bf16[32,16,2048]{2,1,0:T(8,128)(2,1)} %copy-done.7) | copy-start | bytes 6291460
  212.9 57.7 %all-to-all-start.4 = ((bf16[32,16,2048]{2,1,0:T(8,128)(2,1)}), bf16[32,16,2048]{2,1,0:T(8,128)(2,1)}, u32[]{:S(2)}, u32[]{:S(2)}) async-start(bf16[32,16,2048]{2,1,0:T(8,128)(2,1)} %experts.2), calls=%async_computation.4 | async-start | bytes 4194304 | tf_op jit(solution)/shard_map/all_to_all | solution.py:545
  221.7 25.8 %collective-permute-start.6 = (bf16[32,8,2048]{2,1,0:T(8,128)(2,1)S(1)}, bf16[32,8,2048]{2,1,0:T(8,128)(2,1)S(1)}, u32[]{:S(2)}, u32[]{:S(2)}) collective-permute-start(bf16[32,8,2048]{2,1,0:T(8,128)(2,1)S(1)} %get-tuple-element.45), channel_id=1, source_target_pairs={{0,3},{3,0},{1,2},{2,1},{4,7},{7,4},{5,6},{6,5},{8,11},{11,8},{9,1... | collective-permute-start | bytes 3145736 | tf_op jit(solution)/shard_map/ppermute | solution.py:542
  222.6 24.8 %collective-permute-start.7 = (bf16[32,8,2048]{2,1,0:T(8,128)(2,1)S(1)}, bf16[32,8,2048]{2,1,0:T(8,128)(2,1)S(1)}, u32[]{:S(2)}, u32[]{:S(2)}) collective-permute-start(bf16[32,8,2048]{2,1,0:T(8,128)(2,1)S(1)} %get-tuple-element.44), channel_id=1, source_target_pairs={{0,1},{1,0},{2,3},{3,2},{4,5},{5,4},{6,7},{7,6},{8,9},{9,8},{10,11... | collective-permute-start | bytes 3145736 | tf_op jit(solution)/shard_map/ppermute | solution.py:542
  225.8 53.8 %collective-permute-start.12 = (bf16[32,8,2048]{2,1,0:T(8,128)(2,1)}, bf16[32,8,2048]{2,1,0:T(8,128)(2,1)S(1)}, u32[]{:S(2)}, u32[]{:S(2)}) collective-permute-start(bf16[32,8,2048]{2,1,0:T(8,128)(2,1)} %get-tuple-element.43), channel_id=1, source_target_pairs={{0,3},{3,0},{1,2},{2,1},{4,7},{7,4},{5,6},{6,5},{8,11},{11,8},{9,1... | collective-permute-start | bytes 3145736 | tf_op jit(solution)/shard_map/ppermute | solution.py:542
  227.6 52.0 %collective-permute-start.13 = (bf16[32,8,2048]{2,1,0:T(8,128)(2,1)}, bf16[32,8,2048]{2,1,0:T(8,128)(2,1)}, u32[]{:S(2)}, u32[]{:S(2)}) collective-permute-start(bf16[32,8,2048]{2,1,0:T(8,128)(2,1)} %get-tuple-element.42), channel_id=1, source_target_pairs={{0,1},{1,0},{2,3},{3,2},{4,5},{5,4},{6,7},{7,6},{8,9},{9,8},{10,11... | collective-permute-start | bytes 3145736 | tf_op jit(solution)/shard_map/ppermute | solution.py:542
  270.6 49.8 %all-to-all-start.6 = ((bf16[32,16,2048]{2,1,0:T(8,128)(2,1)}), bf16[32,16,2048]{2,1,0:T(8,128)(2,1)S(1)}, u32[]{:S(2)}, u32[]{:S(2)}) async-start(bf16[32,16,2048]{2,1,0:T(8,128)(2,1)} %get-tuple-element.33), calls=%async_computation.6 | async-start | bytes 4194304 | tf_op jit(solution)/shard_map/all_to_all | solution.py:545
  285.5 32.8 %copy-start.2 = (bf16[32,16,2048]{2,1,0:T(8,128)(2,1)S(1)}, bf16[32,16,2048]{2,1,0:T(8,128)(2,1)}, u32[]{:S(2)}) copy-start(bf16[32,16,2048]{2,1,0:T(8,128)(2,1)} %get-tuple-element.38.own) | copy-start | bytes 6291460
  292.3 25.8 %collective-permute-start.14 = (bf16[256,2048]{1,0:T(8,128)(2,1)S(1)}, bf16[256,2048]{1,0:T(8,128)(2,1)S(1)}, u32[]{:S(2)}, u32[]{:S(2)}) collective-permute-start(bf16[256,2048]{1,0:T(8,128)(2,1)S(1)} %get-tuple-element.40), channel_id=1, source_target_pairs={{0,3},{3,0},{1,2},{2,1},{4,7},{7,4},{5,6},{6,5},{8,11},{11,8},{9,1... | collective-permute-start | bytes 3145736 | tf_op jit(solution)/shard_map/ppermute | solution.py:572
  294.1 24.2 %collective-permute-start.15 = (bf16[256,2048]{1,0:T(8,128)(2,1)S(1)}, bf16[256,2048]{1,0:T(8,128)(2,1)S(1)}, u32[]{:S(2)}, u32[]{:S(2)}) collective-permute-start(bf16[256,2048]{1,0:T(8,128)(2,1)S(1)} %get-tuple-element.41), channel_id=1, source_target_pairs={{0,1},{1,0},{2,3},{3,2},{4,5},{5,4},{6,7},{7,6},{8,9},{9,8},{10,11... | collective-permute-start | bytes 3145736 | tf_op jit(solution)/shard_map/ppermute | solution.py:572
  320.4 9.9 %copy-start.20 = (bf16[256,128]{1,0:T(8,128)(2,1)S(1)}, bf16[256,128]{1,0:T(8,128)(2,1)}, u32[]{:S(2)}) copy-start(bf16[256,128]{1,0:T(8,128)(2,1)} %get-tuple-element.35) | copy-start | bytes 196612
  320.4 37.0 %all-to-all-start.7 = ((bf16[32,16,2048]{2,1,0:T(8,128)(2,1)}), bf16[32,16,2048]{2,1,0:T(8,128)(2,1)}, u32[]{:S(2)}, u32[]{:S(2)}) async-start(bf16[32,16,2048]{2,1,0:T(8,128)(2,1)} %merge.1), calls=%async_computation.7 | async-start | bytes 4194304 | tf_op jit(solution)/shard_map/all_to_all | solution.py:545
  329.0 4.8 %collective-permute-start.8 = (bf16[256,128]{1,0:T(8,128)(2,1)S(1)}, bf16[256,128]{1,0:T(8,128)(2,1)S(1)}, u32[]{:S(2)}, u32[]{:S(2)}) collective-permute-start(bf16[256,128]{1,0:T(8,128)(2,1)S(1)} %copy-done.21), channel_id=1, source_target_pairs={{0,3},{3,0},{1,2},{2,1},{4,7},{7,4},{5,6},{6,5},{8,11},{11,8},{9,1... | collective-permute-start | bytes 196616 | tf_op jit(solution)/shard_map/ppermute | solution.py:512
  330.3 3.5 collective-permute-start.9
  335.1 13.5 %collective-permute-start.10 = (bf16[128,2048]{1,0:T(8,128)(2,1)S(1)}, bf16[128,2048]{1,0:T(8,128)(2,1)S(1)}, u32[]{:S(2)}, u32[]{:S(2)}) collective-permute-start(bf16[128,2048]{1,0:T(8,128)(2,1)S(1)} %get-tuple-element.36), channel_id=1, source_target_pairs={{0,3},{3,0},{1,2},{2,1},{4,7},{7,4},{5,6},{6,5},{8,11},{11,8},{9,1... | collective-permute-start | bytes 1572872 | tf_op jit(solution)/shard_map/ppermute | solution.py:566
  336.6 12.0 %collective-permute-start.11 = (bf16[128,2048]{1,0:T(8,128)(2,1)S(1)}, bf16[128,2048]{1,0:T(8,128)(2,1)S(1)}, u32[]{:S(2)}, u32[]{:S(2)}) collective-permute-start(bf16[128,2048]{1,0:T(8,128)(2,1)S(1)} %get-tuple-element.37), channel_id=1, source_target_pairs={{0,1},{1,0},{2,3},{3,2},{4,5},{5,4},{6,7},{7,6},{8,9},{9,8},{10,11... | collective-permute-start | bytes 1572872 | tf_op jit(solution)/shard_map/ppermute | solution.py:567
  (13 other events, 67.0 us)
